TPU v7x, 512 devices: a whole 4x8x8 slice. The times are simulated.
512 devices in a mesh: sky: 64 (over z, y_hi, core), ccd: 8 (over x, y_lo).
Axes of the slice: x: 4, y: 8 (y_hi: 4, y_lo: 2; y = y_hi * 2 + y_lo), z: 8, core: 2. Of those that a mesh axis runs over, the one named last changes fastest.
Arguments:
- science: bfloat16 [384, 1024, 256], P('sky', 'ccd'), may hold values from -6 to 6
- templates: bfloat16 [1024, 1024, 128], P('sky', 'ccd'), may hold values from -6 to 6
- cell_owner: int32 [64, 288, 1], P('sky', 'ccd'), may hold values from 0 to 63; in each aligned block of 36 rows (0 to 35, 36 to 71, ..., all dimensions but the last counted through in order) at most 2 rows name the same one
- cell_index: int32 [64, 288], P('sky', 'ccd'), may hold values from 0 to 15
- row_offset: int32 [384, 8], P('sky', 'ccd'), may hold values from 0 to 98
- col_offset: int32 [384, 8], P('sky', 'ccd'), may hold values from 0 to 98
- coefficients: float32 [384, 8, 21, 6], P('sky', 'ccd'), may hold values from -1.8 to 1.8
- psf_taps: bfloat16 [384, 2, 31], P('sky'), may hold values from 0.029907227 to 0.29882812
Outputs:
- difference: bfloat16 [384, 1024, 256], P('sky', 'ccd')
- score: float32 [384, 1024, 256], P('sky', 'ccd')
Inputs may be any that keep to these rules, and one draw needn't show every extreme that they name: `cell_owner`: within the rows of one device, no owner appears more than 2 times.
All inputs are finite; a program needn't handle non-finite values.
Results may differ from a plain program's by a relative error of at most 0.0062.
Values may be sent and summed in bfloat16 or wider, within the bound.
No kernel may reach another device: no remote copies, remote signals or barrier semaphores. Data moves between devices by JAX's collectives and lax.ppermute only.
A program may use at most 128 MiB of HBM per device.

v0:
```python
import jax
import jax.numpy as jnp
from jax import lax
from jax.sharding import PartitionSpec as P

RAD = 15


basis_width = 4.0


def padded(cells, sides, width):
    for axis, dim in sides:
        count = lax.axis_size(axis)
        ends = count - 1
        head = lax.slice_in_dim(cells, 0, width, axis=dim)
        tail = lax.slice_in_dim(cells, cells.shape[dim] - width, cells.shape[dim], axis=dim)
        cells = jnp.concatenate(
            [
                lax.ppermute(tail, axis, [(i, (i + 1) % count) for i in range(ends)]),
                cells,
                lax.ppermute(head, axis, [((i + 1) % count, i) for i in range(ends)]),
            ],
            axis=dim,
        )
    return cells


def hermite_taps():
    scaled = (jnp.arange(2 * RAD + 1, dtype=jnp.float32) - RAD) / basis_width
    series = [jnp.ones(scaled.shape, jnp.float32), 2.0 * scaled]
    for degree in range(1, 5):
        series.append(2.0 * scaled * series[degree] - 2.0 * degree * series[degree - 1])
    weighted = jnp.stack(series) * jnp.exp(-0.5 * scaled * scaled)
    weighted = weighted / jnp.sqrt(jnp.sum(weighted * weighted, axis=1, keepdims=True))
    return weighted.astype(jnp.bfloat16)


def band_matrix(tap_table, count_in, count_out, tap_shift):
    lag_grid = (
        jnp.arange(count_in, dtype=jnp.int32)[None, :]
        - jnp.arange(count_out, dtype=jnp.int32)[:, None]
        + tap_shift
    )
    hit_grid = (
        lag_grid[:, :, None] == jnp.arange(tap_table.shape[-1], dtype=jnp.int32)[None, None, :]
    ).astype(jnp.bfloat16)
    return jnp.einsum(
        "oiu,ku->koi", hit_grid, tap_table, preferred_element_type=jnp.float32
    ).astype(jnp.bfloat16)


def poly_grid(row_count, col_count):
    row_pos = (2.0 * jnp.arange(row_count, dtype=jnp.float32) + 1.0) / row_count - 1.0
    col_pos = (2.0 * jnp.arange(col_count, dtype=jnp.float32) + 1.0) / col_count - 1.0
    across_pos = jnp.broadcast_to(col_pos[None, :], (row_count, col_count))
    down_pos = jnp.broadcast_to(row_pos[:, None], (row_count, col_count))
    return jnp.stack(
        [
            jnp.ones_like(across_pos),
            across_pos,
            down_pos,
            across_pos * across_pos,
            across_pos * down_pos,
            down_pos * down_pos,
        ]
    )


def slot_rank(row_list, sky_count):
    hit_grid = (row_list[:, None] == jnp.arange(sky_count, dtype=jnp.int32)[None, :]).astype(
        jnp.int32
    )
    earlier = jnp.cumsum(hit_grid, axis=0) - hit_grid
    return jnp.sum(earlier * hit_grid, axis=1)


def pack_requests(owners, indices, slot_ids, sky_count, capacity):
    matched = (owners[:, None, None] == jnp.arange(sky_count, dtype=jnp.int32)[None, :, None]) & (
        slot_ids[:, None, None] == jnp.arange(capacity, dtype=jnp.int32)[None, None, :]
    )
    return jnp.sum(jnp.where(matched, indices[:, None, None] + 1, 0), axis=0) - 1


def body(
    science, templates, cell_owner, cell_index, row_offset, col_offset, coefficients, psf_taps
):
    sky_count = lax.axis_size("sky")
    visit_count, tile_rows, tile_cols = science.shape
    cell_side = templates.shape[2]
    owners = cell_owner[0, :, 0]
    indices = cell_index[0]
    request_count = owners.shape[0]
    capacity = max(2, request_count // sky_count + 1)
    cell_rows = (tile_rows + 2 * RAD) // cell_side + 1
    cell_cols = (tile_cols + 2 * RAD) // cell_side + 1
    slot_ids = slot_rank(owners, sky_count)
    requests = pack_requests(owners, indices, slot_ids, sky_count, capacity)
    wanted = lax.all_to_all(requests, "sky", split_axis=0, concat_axis=0, tiled=True)
    picked = jnp.take(templates, jnp.maximum(wanted, 0), axis=0)
    arrived = lax.all_to_all(
        jnp.where((wanted >= 0)[..., None, None], picked, jnp.zeros_like(picked)),
        "sky",
        split_axis=0,
        concat_axis=0,
        tiled=True,
    )
    flat_ids = owners * capacity + slot_ids
    cell_stack = jnp.take(
        arrived.reshape(sky_count * capacity, cell_side, cell_side), flat_ids, axis=0
    )
    assembled = (
        cell_stack.reshape(visit_count, cell_rows, cell_cols, cell_side, cell_side)
        .transpose(0, 1, 3, 2, 4)
        .reshape(visit_count, cell_rows * cell_side, cell_cols * cell_side)
    )

    def crop_window(image_plane, top_row, left_col):
        return lax.dynamic_slice(
            image_plane, (top_row, left_col), (tile_rows + 2 * RAD, tile_cols + 2 * RAD)
        )

    windows = jax.vmap(crop_window)(assembled, row_offset[:, 0], col_offset[:, 0])
    hermite = hermite_taps()
    across_bands = band_matrix(hermite, tile_cols + 2 * RAD, tile_cols, 0)
    down_bands = band_matrix(hermite, tile_rows + 2 * RAD, tile_rows, 0)
    across = jnp.einsum(
        "vyw,ixw->ivyx", windows, across_bands, preferred_element_type=jnp.float32
    ).astype(jnp.bfloat16)
    poly_terms = poly_grid(tile_rows, tile_cols)
    coef_rows = coefficients[:, 0]
    model_image = jnp.zeros((visit_count, tile_rows, tile_cols), jnp.float32)
    basis_start = 0
    for hx_order in range(6):
        keep_count = 6 - hx_order
        down_pass = jnp.einsum(
            "jyz,vzx->jvyx",
            down_bands[:keep_count],
            across[hx_order],
            preferred_element_type=jnp.float32,
        )
        coef_slice = jnp.transpose(coef_rows[:, basis_start : basis_start + keep_count], (1, 0, 2))
        coef_maps = jnp.sum(coef_slice[:, :, :, None, None] * poly_terms[None, None], axis=2)
        model_image = model_image + jnp.sum(coef_maps * down_pass, axis=0)
        basis_start = basis_start + keep_count
    difference = (science.astype(jnp.float32) - model_image).astype(jnp.bfloat16)
    col_bands = band_matrix(psf_taps[:, 1], tile_cols, tile_cols, RAD)
    row_bands = band_matrix(psf_taps[:, 0], tile_rows + 2 * RAD, tile_rows, 0)
    extended = padded(difference, (("ccd", 1),), RAD)
    filtered = jnp.einsum(
        "vyw,vxw->vyx", extended, col_bands, preferred_element_type=jnp.float32
    ).astype(jnp.bfloat16)
    score_image = jnp.einsum(
        "vyz,vzx->vyx", row_bands, filtered, preferred_element_type=jnp.float32
    )
    return (difference, score_image)


def solution(mesh):
    in_specs = (
        P("sky", "ccd", None),
        P("sky", "ccd", None),
        P("sky", "ccd", None),
        P("sky", "ccd"),
        P("sky", "ccd"),
        P("sky", "ccd"),
        P("sky", "ccd", None, None),
        P("sky", None, None),
    )
    out_specs = (P("sky", "ccd", None), P("sky", "ccd", None))
    return jax.shard_map(body, mesh=mesh, in_specs=in_specs, out_specs=out_specs, check_vma=False)
```

profile of v0, /device:TPU:11, one launch (start us, length us, event | category | flops | bytes accessed | tf_op | source)
XLA Modules:
  0.0 219.7 jit_solution(3951213966046935365)
XLA Ops:
  3.3 27.5 %all_to_all.11 = s32[64,1,2]{2,1,0:T(1,128)S(1)} all-to-all(s32[64,1,2]{2,1,0:T(1,128)S(1)} %copy.84), channel_id=1, replica_groups=mesh['sky'=64,'ccd'=8] {'sky'}, dimensions={0} | all-to-all | bytes 1024 | tf_op jit(solution)/shard_map/all_to_all | solution.py:99
  31.4 3.0 %gather_fusion = bf16[128,128,128]{2,1,0:T(8,128)(2,1)} fusion(bf16[16,128,128]{2,1,0:T(8,128)(2,1)S(1)} %copy-done, s32[1024]{0:T(1024)S(1)} %pad_clamp_fusion.1), kind=kCustom, calls=%fused_computation | custom fusion | bytes 8389120 | tf_op jit(solution)/shard_map/jit(_take)/gather | solution.py:100
  34.5 4.0 %select_select_fusion = bf16[64,2,128,128]{3,2,1,0:T(8,128)(2,1)} fusion(bf16[64,2,128,128]{3,2,1,0:T(8,128)(2,1)} %bitcast.166, pred[64,2]{1,0:T(8,128)(4,1)S(1)} %copy.88, pred[64,2]{1,0:T(8,128)(4,1)S(1)} %copy.86), kind=kLoop, calls=%fused_computation.18 | loop fusion | flops 4194304 | bytes 8388864 | tf_op jit(solution)/shard_map/jit(_where)/select_n | solution.py:102
  38.5 5.8 %all-to-all-start.1 = ((bf16[64,2,128,128]{3,2,1,0:T(8,128)(2,1)}), bf16[64,2,128,128]{3,2,1,0:T(8,128)(2,1)}, u32[]{:S(2)}, u32[]{:S(2)}) async-start(bf16[64,2,128,128]{3,2,1,0:T(8,128)(2,1)} %select_select_fusion), calls=%async_computation.1 | async-start | bytes 8388608 | tf_op jit(solution)/shard_map/all_to_all | solution.py:101
  47.4 4.7 %multiply_reduce_fusion = f32[6,6,128,256]{3,2,1,0:T(8,128)} fusion(f32[6,128,256]{2,1,0:T(8,128)S(1)} %broadcast_dynamic-update-slice_fusion, f32[6,6,6]{2,1,0:T(8,128)S(1)} %slice_bitcast_fusion.12), kind=kLoop, calls=%fused_computation.4 | loop fusion | flops 12976128 | bytes 5505888 | tf_op jit(solution)/shard_map/reduce_sum | solution.py:143
  52.0 6.0 %copy.94 = f32[6,6,128,256]{2,3,0,1:T(8,128)} copy(f32[6,6,128,256]{3,2,1,0:T(8,128)} %multiply_reduce_fusion) | data formatting | bytes 9437184 | tf_op jit(solution)/shard_map/reduce_sum | solution.py:143
  58.1 4.0 %multiply_reduce_fusion.1 = f32[5,6,128,256]{3,2,1,0:T(8,128)} fusion(f32[6,128,256]{2,1,0:T(8,128)S(1)} %broadcast_dynamic-update-slice_fusion, f32[5,6,6]{2,1,0:T(8,128)S(1)} %slice_bitcast_fusion.13), kind=kLoop, calls=%fused_computation.5 | loop fusion | flops 10813440 | bytes 4719312 | tf_op jit(solution)/shard_map/reduce_sum | solution.py:143
  62.1 5.5 %copy.96 = f32[5,6,128,256]{2,3,0,1:T(8,128)} copy(f32[5,6,128,256]{3,2,1,0:T(8,128)} %multiply_reduce_fusion.1) | data formatting | bytes 7864320 | tf_op jit(solution)/shard_map/reduce_sum | solution.py:143
  67.6 3.4 %multiply_reduce_fusion.2 = f32[4,6,128,256]{3,2,1,0:T(8,128)} fusion(f32[6,128,256]{2,1,0:T(8,128)S(1)} %broadcast_dynamic-update-slice_fusion, f32[4,6,6]{2,1,0:T(8,128)S(1)} %slice_bitcast_fusion.14), kind=kLoop, calls=%fused_computation.6 | loop fusion | flops 8650752 | bytes 3932736 | tf_op jit(solution)/shard_map/reduce_sum | solution.py:143
  71.0 3.5 %copy.100 = f32[4,6,128,256]{2,3,0,1:T(8,128)} copy(f32[4,6,128,256]{3,2,1,0:T(8,128)} %multiply_reduce_fusion.2) | data formatting | bytes 6291456 | tf_op jit(solution)/shard_map/reduce_sum | solution.py:143
  74.5 2.7 %multiply_reduce_fusion.3 = f32[3,6,128,256]{3,2,1,0:T(8,128)} fusion(f32[6,128,256]{2,1,0:T(8,128)S(1)} %broadcast_dynamic-update-slice_fusion, f32[3,6,6]{2,1,0:T(8,128)S(1)} %slice_bitcast_fusion.15), kind=kLoop, calls=%fused_computation.7 | loop fusion | flops 6488064 | bytes 3146160 | tf_op jit(solution)/shard_map/reduce_sum | solution.py:143
  77.2 3.1 %copy.103 = f32[3,6,128,256]{2,3,0,1:T(8,128)} copy(f32[3,6,128,256]{3,2,1,0:T(8,128)} %multiply_reduce_fusion.3) | data formatting | bytes 4718592 | tf_op jit(solution)/shard_map/reduce_sum | solution.py:143
  82.8 2.9 %fusion.13 = bf16[6,256,286,1]{1,0,2,3:T(8,128)(2,1)} fusion(s32[256,286]{0,1:T(8,128)S(1)} %iota_subtract_fusion, f32[6,31]{1,0:T(8,128)S(1)} %stack.21, f32[6]{0:T(128)S(1)} %sqrt.8, f32[31]{0:T(128)S(1)} %multiply_exponential_fusion), kind=kOutput, calls=%fused_computation.33 | convolution fusion | flops 29945902 | bytes 1172348 | tf_op jit(solution)/shard_map/oiu,ku->koi/dot_general | solution.py:48
  87.1 2.8 %fusion.14 = bf16[6,256,256]{2,0,1:T(8,128)(2,1)} fusion(s32[256,256]{1,0:T(8,128)S(1)} %subtract_add_fusion, bf16[6,1,31]{2,1,0:T(2,128)(2,1)S(1)} %get-tuple-element.40), kind=kOutput, calls=%fused_computation.34 | convolution fusion | flops 26804224 | bytes 1048948 | tf_op jit(solution)/shard_map/oiu,ku->koi/dot_general | solution.py:48
  89.9 48.0 %all-to-all-done.1 = bf16[64,2,128,128]{3,2,1,0:T(8,128)(2,1)} async-done(((bf16[64,2,128,128]{3,2,1,0:T(8,128)(2,1)}), bf16[64,2,128,128]{3,2,1,0:T(8,128)(2,1)}, u32[]{:S(2)}, u32[]{:S(2)}) %all-to-all-start.1) | async-done | bytes 4194336 | tf_op jit(solution)/shard_map/all_to_all | solution.py:101
  137.9 3.0 %gather_fusion.1 = bf16[36,128,128]{2,1,0:T(8,128)(2,1)S(1)} fusion(bf16[128,128,128]{2,1,0:T(8,128)(2,1)} %bitcast.10, s32[1024]{0:T(1024)S(1)} %pad_clamp_fusion), kind=kCustom, calls=%fused_computation.1 | custom fusion | bytes 2359440 | tf_op jit(solution)/shard_map/jit(_take)/gather | solution.py:109
  143.1 19.1 %while.1 = (s32[]{:T(128)}, bf16[6,256,384]{2,1,0:T(8,128)(2,1)S(1)}, s32[6,3]{0,1:T(4,128)S(1)}, bf16[6,158,286]{2,1,0:T(8,128)(2,1)}, s32[]{:T(128)}) while((s32[]{:T(128)}, bf16[6,256,384]{2,1,0:T(8,128)(2,1)S(1)}, s32[6,3]{0,1:T(4,128)S(1)}, bf16[6,158,286]{2,1,0:T(8,128)(2,1)}, s32[]{:T(128)}) %tuple.35), condition=%wide.while_cond, body=%wide.while_body.sunk | while | flops 2 | bytes 215417 | solution.py:119
  143.7 2.6 %dynamic-slice_dynamic-update-slice_fusion.2 = bf16[6,158,286]{2,1,0:T(8,128)(2,1)} fusion(bf16[6,158,286]{2,1,0:T(8,128)(2,1)} %get-tuple-element.90, s32[]{:T(128)} %get-tuple-element.87, bf16[6,256,384]{2,1,0:T(8,128)(2,1)S(1)} %get-tuple-element.93, s32[]{:T(128)} %bitcast.163, s32[]{:T(128)} %bitcast.164, s32[]{:T(128)} %bitcast.165), kind=kLoop, calls=%fused_computation.2.clone.1 | loop fusion | bytes 215304 | tf_op jit(solution)/shard_map/vmap()/gather
  146.9 2.6 %dynamic-slice_dynamic-update-slice_fusion.2 = bf16[6,158,286]{2,1,0:T(8,128)(2,1)} fusion(bf16[6,158,286]{2,1,0:T(8,128)(2,1)} %get-tuple-element.90, s32[]{:T(128)} %get-tuple-element.87, bf16[6,256,384]{2,1,0:T(8,128)(2,1)S(1)} %get-tuple-element.93, s32[]{:T(128)} %bitcast.163, s32[]{:T(128)} %bitcast.164, s32[]{:T(128)} %bitcast.165), kind=kLoop, calls=%fused_computation.2.clone.1 | loop fusion | bytes 215304 | tf_op jit(solution)/shard_map/vmap()/gather
  150.1 2.6 %dynamic-slice_dynamic-update-slice_fusion.2 = bf16[6,158,286]{2,1,0:T(8,128)(2,1)} fusion(bf16[6,158,286]{2,1,0:T(8,128)(2,1)} %get-tuple-element.90, s32[]{:T(128)} %get-tuple-element.87, bf16[6,256,384]{2,1,0:T(8,128)(2,1)S(1)} %get-tuple-element.93, s32[]{:T(128)} %bitcast.163, s32[]{:T(128)} %bitcast.164, s32[]{:T(128)} %bitcast.165), kind=kLoop, calls=%fused_computation.2.clone.1 | loop fusion | bytes 215304 | tf_op jit(solution)/shard_map/vmap()/gather
  153.3 2.6 %dynamic-slice_dynamic-update-slice_fusion.2 = bf16[6,158,286]{2,1,0:T(8,128)(2,1)} fusion(bf16[6,158,286]{2,1,0:T(8,128)(2,1)} %get-tuple-element.90, s32[]{:T(128)} %get-tuple-element.87, bf16[6,256,384]{2,1,0:T(8,128)(2,1)S(1)} %get-tuple-element.93, s32[]{:T(128)} %bitcast.163, s32[]{:T(128)} %bitcast.164, s32[]{:T(128)} %bitcast.165), kind=kLoop, calls=%fused_computation.2.clone.1 | loop fusion | bytes 215304 | tf_op jit(solution)/shard_map/vmap()/gather
  156.5 2.6 %dynamic-slice_dynamic-update-slice_fusion.2 = bf16[6,158,286]{2,1,0:T(8,128)(2,1)} fusion(bf16[6,158,286]{2,1,0:T(8,128)(2,1)} %get-tuple-element.90, s32[]{:T(128)} %get-tuple-element.87, bf16[6,256,384]{2,1,0:T(8,128)(2,1)S(1)} %get-tuple-element.93, s32[]{:T(128)} %bitcast.163, s32[]{:T(128)} %bitcast.164, s32[]{:T(128)} %bitcast.165), kind=kLoop, calls=%fused_computation.2.clone.1 | loop fusion | bytes 215304 | tf_op jit(solution)/shard_map/vmap()/gather
  159.7 2.6 %dynamic-slice_dynamic-update-slice_fusion.2 = bf16[6,158,286]{2,1,0:T(8,128)(2,1)} fusion(bf16[6,158,286]{2,1,0:T(8,128)(2,1)} %get-tuple-element.90, s32[]{:T(128)} %get-tuple-element.87, bf16[6,256,384]{2,1,0:T(8,128)(2,1)S(1)} %get-tuple-element.93, s32[]{:T(128)} %bitcast.163, s32[]{:T(128)} %bitcast.164, s32[]{:T(128)} %bitcast.165), kind=kLoop, calls=%fused_computation.2.clone.1 | loop fusion | bytes 215304 | tf_op jit(solution)/shard_map/vmap()/gather
  162.2 3.2 %convert_bitcast_fusion = bf16[6,6,158,256]{3,2,1,0:T(8,128)(2,1)S(1)} fusion(bf16[6,256,286,1]{1,0,2,3:T(8,128)(2,1)} %fusion.13, bf16[6,158,286]{2,1,0:T(8,128)(2,1)} %get-tuple-element.9), kind=kOutput, calls=%fused_computation.23 | convolution fusion | flops 834361344 | bytes 4333104 | tf_op jit(solution)/shard_map/vyw,ixw->ivyx/dot_general | solution.py:127
  167.1 3.2 %fusion.2 = f32[6,128,256]{1,2,0:T(8,128)S(1)} fusion(f32[6,6,128,256]{2,3,0,1:T(8,128)} %copy.94, bf16[6,6,158,256]{3,2,1,0:T(8,128)(2,1)S(1)} %convert_bitcast_fusion, bf16[6,128,158]{1,0,2:T(8,128)(2,1)S(1)} %fusion.23), kind=kOutput, calls=%fused_computation.14 | convolution fusion | flops 374931456 | bytes 6320128 | tf_op jit(solution)/shard_map/jyz,vzx->jvyx/dot_general | solution.py:136
  171.5 3.2 %fusion.5 = f32[6,128,256]{1,2,0:T(8,128)S(1)} fusion(f32[5,6,128,256]{2,3,0,1:T(8,128)} %copy.96, bf16[6,6,158,256]{3,2,1,0:T(8,128)(2,1)} %copy-done.5, bf16[5,128,158]{1,0,2:T(8,128)(2,1)S(1)} %bitcast.168), kind=kOutput, calls=%fused_computation.20 | convolution fusion | flops 312410112 | bytes 5412352 | tf_op jit(solution)/shard_map/jyz,vzx->jvyx/dot_general | solution.py:136
  175.8 3.8 %fusion.6 = f32[6,128,256]{1,2,0:T(8,128)} fusion(f32[4,6,128,256]{2,3,0,1:T(8,128)} %copy.100, bf16[6,6,158,256]{3,2,1,0:T(8,128)(2,1)} %copy-done.5, bf16[4,128,158]{1,0,2:T(4,128)(2,1)S(1)} %slice.109), kind=kOutput, calls=%fused_computation.22 | convolution fusion | flops 249888768 | bytes 4585472 | tf_op jit(solution)/shard_map/jyz,vzx->jvyx/dot_general | solution.py:136
  181.9 2.6 %fusion.9 = f32[6,128,256]{1,2,0:T(8,128)} fusion(f32[3,6,128,256]{2,3,0,1:T(8,128)S(1)} %copy-done.2, bf16[6,6,158,256]{3,2,1,0:T(8,128)(2,1)} %copy-done.5, bf16[3,128,158]{1,0,2:T(4,128)(2,1)S(1)} %slice.112), kind=kOutput, calls=%fused_computation.28 | convolution fusion | flops 187367424 | bytes 3758592 | tf_op jit(solution)/shard_map/jyz,vzx->jvyx/dot_general | solution.py:136
  190.2 2.5 %fusion.21 = bf16[6,128,256]{2,1,0:T(8,128)(2,1)S(1)} fusion(f32[6,128,256]{2,1,0:T(8,128)S(1)} %copy-done.3, f32[6,128,256]{2,1,0:T(8,128)} %copy.107, f32[6,128,256]{2,1,0:T(8,128)} %copy.104, f32[6,128,256]{2,1,0:T(8,128)} %copy.101, f32[6,128,256]{2,1,0:T(8,128)S(1)} %copy-done.4, f32[6,128,256]{2,1,0:T(8,128)} %copy.98, ...), kind=kOutput, calls=%fused_computation.43 | convolution fusion | flops 63897600 | bytes 6036992 | tf_op jit(solution)/shard_map/jyz,vzx->jvyx/dot_general | solution.py:136
  192.8 17.9 %collective-permute-start = (bf16[6,15,256]{2,1,0:T(8,128)(2,1)S(1)}, bf16[6,15,256]{2,1,0:T(8,128)(2,1)S(1)}, u32[]{:S(2)}, u32[]{:S(2)}) collective-permute-start(bf16[6,15,256]{2,1,0:T(8,128)(2,1)S(1)} %get-tuple-element.37), channel_id=1, source_target_pairs={{0,1},{1,2},{2,3},{3,4},{4,5},{5,6},{6,7},{8,9},{9,10},{10,11},{11... | collective-permute-start | bytes 138248 | tf_op jit(solution)/shard_map/ppermute | solution.py:20
  213.3 3.8 %collective-permute-done.1 = bf16[6,15,256]{2,1,0:T(8,128)(2,1)S(1)} collective-permute-done((bf16[6,15,256]{2,1,0:T(8,128)(2,1)S(1)}, bf16[6,15,256]{2,1,0:T(8,128)(2,1)S(1)}, u32[]{:S(2)}, u32[]{:S(2)}) %collective-permute-start.1) | collective-permute-done | bytes 46112 | tf_op jit(solution)/shard_map/ppermute | solution.py:22
  217.0 2.7 %fusion.22 = f32[6,128,256]{2,1,0:T(8,128)} fusion(bf16[6,256,256]{2,0,1:T(8,128)(2,1)} %fusion.14, bf16[6,15,256]{2,1,0:T(8,128)(2,1)S(1)} %collective-permute-done.1, bf16[6,128,256]{2,1,0:T(8,128)(2,1)S(1)} %fusion.21, bf16[6,15,256]{2,1,0:T(8,128)(2,1)S(1)} %collective-permute-done, bf16[6,128,158]{1,0,2:T(8,128)(2,1)S(1)} %fusion.25), kind=kOutput, calls=%fused_computation.44 | convolution fusion | flops 188083200 | bytes 2300928 | tf_op jit(solution)/shard_map/vyz,vzx->vyx/dot_general | solution.py:153
  (120 shorter events, 30.5 us)
Async XLA Ops:
  0.6 30.8 %copy-start = (bf16[16,128,128]{2,1,0:T(8,128)(2,1)S(1)}, bf16[16,128,128]{2,1,0:T(8,128)(2,1)}, u32[]{:S(2)}) copy-start(bf16[16,128,128]{2,1,0:T(8,128)(2,1)} %param.9) | copy-start | bytes 1572868
  38.4 8.3 %copy-start.13 = (s32[1,36,1]{1,2,0:T(1,128)S(1)}, s32[1,36,1]{1,2,0:T(1,128)}, u32[]{:S(2)}) copy-start(s32[1,36,1]{1,2,0:T(1,128)} %param.10) | copy-start | bytes 436
  38.5 8.4 %copy-start.11 = (f32[6,1,21,6]{2,1,3,0:T(1,128)S(1)}, f32[6,1,21,6]{2,1,3,0:T(1,128)}, u32[]{:S(2)}) copy-start(f32[6,1,21,6]{2,1,3,0:T(1,128)} %param.14) | copy-start | bytes 9076
  38.5 99.4 %all-to-all-start.1 = ((bf16[64,2,128,128]{3,2,1,0:T(8,128)(2,1)}), bf16[64,2,128,128]{3,2,1,0:T(8,128)(2,1)}, u32[]{:S(2)}, u32[]{:S(2)}) async-start(bf16[64,2,128,128]{3,2,1,0:T(8,128)(2,1)} %select_select_fusion), calls=%async_computation.1 | async-start | bytes 8388608 | tf_op jit(solution)/shard_map/all_to_all | solution.py:101
  44.6 0.6 copy-start.9
  80.3 2.4 %copy-start.14 = (s32[6,1]{0,1:T(1,128)S(1)}, s32[6,1]{0,1:T(1,128)}, u32[]{:S(2)}) copy-start(s32[6,1]{0,1:T(1,128)} %param.13) | copy-start | bytes 76
  80.3 2.4 %copy-start.15 = (s32[6,1]{0,1:T(1,128)S(1)}, s32[6,1]{0,1:T(1,128)}, u32[]{:S(2)}) copy-start(s32[6,1]{0,1:T(1,128)} %param.12) | copy-start | bytes 76
  81.0 6.0 %copy-start.12 = (bf16[6,2,31]{2,1,0:T(2,128)(2,1)S(1)}, bf16[6,2,31]{2,1,0:T(2,128)(2,1)}, u32[]{:S(2)}) copy-start(bf16[6,2,31]{2,1,0:T(2,128)(2,1)} %param.15) | copy-start | bytes 2236
  165.4 1.7 copy-start.5
  175.8 6.1 %copy-start.2 = (f32[3,6,128,256]{2,3,0,1:T(8,128)S(1)}, f32[3,6,128,256]{2,3,0,1:T(8,128)}, u32[]{:S(2)}) copy-start(f32[3,6,128,256]{2,3,0,1:T(8,128)} %copy.103) | copy-start | bytes 7077892
  184.5 5.7 %copy-start.3 = (f32[6,128,256]{2,1,0:T(8,128)S(1)}, f32[6,128,256]{2,1,0:T(8,128)}, u32[]{:S(2)}) copy-start(f32[6,128,256]{2,1,0:T(8,128)} %multiply_reduce_fusion.5) | copy-start | bytes 2359300
  184.5 5.7 %copy-start.4 = (f32[6,128,256]{2,1,0:T(8,128)S(1)}, f32[6,128,256]{2,1,0:T(8,128)}, u32[]{:S(2)}) copy-start(f32[6,128,256]{2,1,0:T(8,128)} %copy.97) | copy-start | bytes 2359300
  184.5 5.7 %copy-start.7 = (bf16[6,128,256]{2,1,0:T(8,128)(2,1)S(1)}, bf16[6,128,256]{2,1,0:T(8,128)(2,1)}, u32[]{:S(2)}) copy-start(bf16[6,128,256]{2,1,0:T(8,128)(2,1)} %param.8) | copy-start | bytes 1179652
  184.5 5.7 %copy-start.8 = (bf16[1,128,158]{1,0,2:T(2,128)(2,1)S(1)}, bf16[1,128,158]{1,0,2:T(2,128)(2,1)}, u32[]{:S(2)}) copy-start(bf16[1,128,158]{1,0,2:T(2,128)(2,1)} %slice.118) | copy-start | bytes 121348
  190.2 22.5 %copy-start.10 = (s32[128,158]{0,1:T(8,128)S(1)}, s32[128,158]{0,1:T(8,128)}, u32[]{:S(2)}) copy-start(s32[128,158]{0,1:T(8,128)} %copy-done.9) | copy-start | bytes 242692
  190.2 29.5 %copy-start.1 = (bf16[16,128,128]{2,1,0:T(8,128)(2,1)S(1)}, bf16[16,128,128]{2,1,0:T(8,128)(2,1)}, u32[]{:S(2)}) copy-start(bf16[16,128,128]{2,1,0:T(8,128)(2,1)} %param.9) | copy-start | bytes 1572868
  192.8 27.0 %copy-start.6 = (bf16[6,128,256]{2,1,0:T(8,128)(2,1)}, bf16[6,128,256]{2,1,0:T(8,128)(2,1)S(1)}, u32[]{:S(2)}) copy-start(bf16[6,128,256]{2,1,0:T(8,128)(2,1)S(1)} %fusion.21) | copy-start | bytes 1179652
  192.8 20.5 %collective-permute-start = (bf16[6,15,256]{2,1,0:T(8,128)(2,1)S(1)}, bf16[6,15,256]{2,1,0:T(8,128)(2,1)S(1)}, u32[]{:S(2)}, u32[]{:S(2)}) collective-permute-start(bf16[6,15,256]{2,1,0:T(8,128)(2,1)S(1)} %get-tuple-element.37), channel_id=1, source_target_pairs={{0,1},{1,2},{2,3},{3,4},{4,5},{5,6},{6,7},{8,9},{9,10},{10,11},{11... | collective-permute-start | bytes 138248 | tf_op jit(solution)/shard_map/ppermute | solution.py:20
  210.7 6.3 %collective-permute-start.1 = (bf16[6,15,256]{2,1,0:T(8,128)(2,1)S(1)}, bf16[6,15,256]{2,1,0:T(8,128)(2,1)S(1)}, u32[]{:S(2)}, u32[]{:S(2)}) collective-permute-start(bf16[6,15,256]{2,1,0:T(8,128)(2,1)S(1)} %get-tuple-element.38), channel_id=1, source_target_pairs={{1,0},{2,1},{3,2},{4,3},{5,4},{6,5},{7,6},{9,8},{10,9},{11,10},{12... | collective-permute-start | bytes 138248 | tf_op jit(solution)/shard_map/ppermute | solution.py:22
where the time goes:
time: 221 us; the launch traced here: 220 us
  local copies, waits for them, and re-layouts  59.6 us (27%)
  waiting for transfers between devices  51.7 us (23%)
  matrix products  30.1 us (14%)
  blocking collectives  27.5 us (12%)
  starting transfers between devices  25.6 us (12%)
  other arithmetic  24 us (11%)
    all_to_all x1, waiting for transfers between devices, body(): lax.all_to_all(jnp.where((wanted >= 0)[..., None, None], picked, jnp.zero...  48 us
    all_to_all x1, blocking collectives, body(): lax.all_to_all(requests, 'sky', split_axis=0, concat_axis=0, tiled=True)  27.5 us
    reduce_sum x5, local copies, waits for them, and re-layouts, body(): jnp.sum(coef_slice[:, :, :, None, None] * poly_terms[None, None], axis=2)  19.7 us
    gather x18, local copies, waits for them, and re-layouts  19.1 us
    ppermute x1, starting transfers between devices, padded(): lax.ppermute(tail, axis, [(i, (i + 1) % count) for i in range(ends)])  17.9 us
    dot_general x6, matrix products, body(): jnp.einsum('jyz,vzx->jvyx', down_bands[:keep_count], across[hx_order], pr...  17.3 us
    reduce_sum x6, other arithmetic, body(): jnp.sum(coef_slice[:, :, :, None, None] * poly_terms[None, None], axis=2)  16.8 us
    reduce_sum x5, local copies, waits for them, and re-layouts, body(): model_image = model_image + jnp.sum(coef_maps * down_pass, axis=0)  8.28 us
  transfers between devices with their start and end apart: 3, of which 2 were waited for; matrix products, arithmetic and copies ran while one was open for 21% of the time, Pallas kernels for 0%

commit v1 on v0

v1 whole, which is shorter than its diff:
```python
import jax
import jax.numpy as jnp
import numpy as np
from jax import lax
from jax.experimental import pallas as pl
from jax.experimental.pallas import tpu as pltpu
from jax.sharding import PartitionSpec as P

RAD = 15
TAPS = 31
ORDERS = 6
GROUP = 64
CELLS = 16
SIDE = 128
VISITS = 6
COLS = 256
HALO = 16
STRIPE = 32
PACKED = 40
PICKS = 54
PICKPAD = 56
MAXOFF = 98
FAR = 256
f32 = jnp.float32
bf16 = jnp.bfloat16
VM = pl.BlockSpec(memory_space=pltpu.VMEM)
SM = pl.BlockSpec(memory_space=pltpu.SMEM)


def hermite_table():
    t = (np.arange(TAPS, dtype=np.float32) - np.float32(RAD)) / np.float32(4.0)
    series = [np.ones(t.shape, np.float32), np.float32(2.0) * t]
    for n in range(1, ORDERS - 1):
        series.append(np.float32(2.0) * t * series[n] - np.float32(2.0 * n) * series[n - 1])
    w = np.stack(series) * np.exp(np.float32(-0.5) * t * t)
    w = w / np.sqrt(np.sum(w * w, axis=1, keepdims=True))
    return np.asarray(w, dtype=jnp.bfloat16).astype(np.float32)


def request_selector():
    sel = np.zeros((3 * PICKPAD, 128), np.float32)
    for slot in range(3):
        for v in range(VISITS):
            for b in range(3):
                row = slot * 18 + v * 3 + b
                for late in range(2):
                    a = (0, 1, late)[slot]
                    sel[late * PICKPAD + row, v * 6 + a * 3 + b] = CELLS
                    sel[late * PICKPAD + row, 36 + v * 6 + a * 3 + b] = 1
                sel[2 * PICKPAD + row, 72 + v] = 1
    return sel


def pack_kernel(cells_ref, info_ref, out_ref, wide_ref):
    for k in range(CELLS):
        wide_ref[k * SIDE : (k + 1) * SIDE, :] = cells_ref[k].astype(f32)
    info = jnp.broadcast_to(info_ref[...], (PACKED - STRIPE, 128)).astype(f32)

    def step(d, _):
        low = wide_ref[pl.ds(d, CELLS, stride=SIDE), :]
        high = wide_ref[pl.ds(d + GROUP, CELLS, stride=SIDE), :]
        out_ref[d] = jnp.concatenate([low, high, info], axis=0).astype(bf16)
        return 0

    lax.fori_loop(0, GROUP, step, 0, unroll=8)


def select_kernel(me_ref, stripes_ref, sel_ref, out_ref):
    table = jnp.concatenate(
        [
            stripes_ref[:, 0:CELLS, :].reshape(GROUP * CELLS, 128),
            stripes_ref[:, CELLS:STRIPE, :].reshape(GROUP * CELLS, 128),
        ],
        axis=1,
    )
    info = stripes_ref[:, STRIPE, :]
    info = jnp.concatenate([info, jnp.zeros_like(info)], axis=0)
    seen = lax.dot_general(
        sel_ref[...], info, (((1,), (1,)), ((), ())), preferred_element_type=f32
    )
    late = seen[2 * PICKPAD :] > me_ref[0].astype(f32)
    wanted = jnp.where(late, seen[PICKPAD : 2 * PICKPAD], seen[:PICKPAD])
    slot_row = lax.broadcasted_iota(jnp.int32, (PICKPAD, 128), 0)
    half = jnp.where(slot_row < 18, 1.0, jnp.where(slot_row < 36, 0.0, jnp.where(late, 1.0, 0.0)))
    number = lax.broadcasted_iota(jnp.int32, (PICKPAD, GROUP * CELLS), 1).astype(f32)
    batch = 8

    def step(g, carry):
        want, side = carry
        hot = jnp.concatenate(
            [jnp.where(number == want[:, n : n + 1], 1.0, 0.0) for n in range(batch)], axis=0
        ).astype(bf16)
        got = jnp.dot(hot, table, preferred_element_type=f32)
        for n in range(batch):
            rows = got[n * PICKPAD : (n + 1) * PICKPAD]
            pick = jnp.where(side[:, n : n + 1] > 0.5, rows[:, 128:], rows[:, :128])
            out_ref[g * batch + n] = pick.astype(bf16)
        return pltpu.roll(want, 128 - batch, 1), pltpu.roll(side, 128 - batch, 1)

    lax.fori_loop(0, GROUP // batch, step, (wanted, half))


def bands_kernel(
    oy_ref, ox_ref, coef_ref, taps_ref, rev_ref, psf_ref,
    across_ref, down_ref, colf_ref, rowf_ref, tall_ref, toep_ref, shift_ref,
):
    v = pl.program_id(0)

    def spread(row, count):
        return pltpu.roll(jnp.broadcast_to(row, (count, FAR)), 0, 1, stride=1, stride_axis=0)

    @pl.when(v == 0)
    def _():
        for i in range(ORDERS):
            tall_ref[i] = spread(rev_ref[i : i + 1, :], 360)[:, :128]
            toep_ref[i] = spread(taps_ref[i : i + 1, :], SIDE)

    oy = oy_ref[v]
    ox = ox_ref[v]
    for i in range(ORDERS):
        across_ref[0, :, i * 128 : (i + 1) * 128] = tall_ref[i, pl.ds(MAXOFF - ox, FAR), :].astype(
            bf16
        )
        shift_ref[i] = pltpu.roll(toep_ref[i], oy + 192, 1)
    near = lax.broadcasted_iota(jnp.int32, (COLS, COLS), 0) - lax.broadcasted_iota(
        jnp.int32, (COLS, COLS), 1
    )
    colf_ref[0] = jnp.where(
        jnp.abs(near) <= RAD, spread(psf_ref[0, 0:1, :], COLS), 0.0
    ).astype(bf16)
    rowf_ref[0] = spread(psf_ref[0, 1:2, :], SIDE).astype(bf16)

    left = lax.broadcasted_iota(jnp.int32, (16, 128), 1) < 64

    def step(g, _):
        row = lax.broadcasted_iota(jnp.int32, (16, 128), 0) + g * 16
        ty = (2.0 * row.astype(f32) + 1.0) / SIDE - 1.0
        bands = [shift_ref[j, pl.ds(g * 16, 16), :] for j in range(ORDERS)]
        first = 0
        held = None
        for i in range(ORDERS):
            sums = [None] * 6
            for j in range(ORDERS - i):
                c = [coef_ref[v, (first + j) * 6 + p] for p in range(6)]
                flat = c[0] + ty * (c[2] + ty * c[5])
                slope = c[1] + ty * c[4]
                for part in range(2):
                    band = bands[j][:, part * 128 : (part + 1) * 128]
                    for q, weight in enumerate((flat, slope, c[3])):
                        term = weight * band
                        at = q * 2 + part
                        sums[at] = term if sums[at] is None else sums[at] + term
            first += ORDERS - i
            ends = []
            for q in range(3):
                down_ref[0, pl.ds(q * SIDE + g * 16, 16), i * 128 : (i + 1) * 128] = sums[
                    q * 2
                ].astype(bf16)
                ends.append(sums[q * 2 + 1] + pltpu.roll(sums[q * 2 + 1], 64, 1))
            if i % 2 == 0:
                held = ends
            else:
                at = ORDERS * 128 + (i // 2) * 128
                for q in range(3):
                    down_ref[0, pl.ds(q * SIDE + g * 16, 16), at : at + 128] = jnp.where(
                        left, held[q], ends[q]
                    ).astype(bf16)
        return 0

    lax.fori_loop(0, SIDE // 16, step, 0)


def model_kernel(
    rows_ref, across_ref, down_ref, colf_ref, rowf_ref, sci_ref,
    diff_ref, score_ref, part_ref, top_ref, bot_ref, wide_ref, win_ref, stack_ref,
):
    v = pl.program_id(0)

    @pl.when(v == 0)
    def _():
        wide_ref[...] = rows_ref[...].reshape(GROUP * PICKPAD, 128).astype(f32)
        for slot in range(3):
            for n in range(VISITS):
                for b in range(3):
                    win_ref[n, slot * GROUP : (slot + 1) * GROUP, b * 128 : (b + 1) * 128] = (
                        wide_ref[pl.ds(slot * 18 + n * 3 + b, GROUP, stride=PICKPAD), :]
                    ).astype(bf16)

    for xb in range(2):
        at = xb * 128
        got = jnp.dot(
            win_ref[v, :, at : at + 256], across_ref[0], preferred_element_type=f32
        ).astype(bf16)
        for i in range(ORDERS):
            piece = got[:, i * 128 : (i + 1) * 128]
            stack_ref[i * 128 : (i + 1) * 128, at : at + 128] = piece[0:128]
            low = ORDERS * 128 + i * 64
            stack_ref[low : low + 64, at : at + 128] = piece[128:192]
    parts = jnp.dot(down_ref[0], stack_ref[...], preferred_element_type=f32)
    col = lax.broadcasted_iota(jnp.int32, (SIDE, COLS), 1).astype(f32)
    tx = (2.0 * col + 1.0) / COLS - 1.0
    model = parts[0:128] + tx * (parts[128:256] + tx * parts[256:384])
    diff = (sci_ref[0].astype(f32) - model).astype(bf16)
    diff_ref[0] = diff
    filt = jnp.dot(diff, colf_ref[0], preferred_element_type=f32).astype(bf16)
    top_ref[0] = filt[0:HALO]
    bot_ref[0] = filt[SIDE - HALO :]
    score = jnp.dot(rowf_ref[0, :, 0:128], filt, preferred_element_type=f32)
    score_ref[0] = score
    part_ref[0, 0:HALO] = score[0:HALO]
    part_ref[0, HALO:] = score[SIDE - HALO :]


def edge_kernel(part_ref, above_ref, below_ref, rowf_ref, _, score_ref, buf_ref, sem):
    for v in range(VISITS):
        gap = jnp.zeros((128 - 2 * HALO, COLS), bf16)
        ring = jnp.concatenate([below_ref[v], gap, above_ref[v]], axis=0)
        band = jnp.concatenate(
            [rowf_ref[v, 0:HALO, 128:256], rowf_ref[v, SIDE - HALO :, 128:256]], axis=0
        )
        buf_ref[v] = part_ref[v] + jnp.dot(band, ring, preferred_element_type=f32)
    top = pltpu.make_async_copy(buf_ref.at[:, 0:HALO], score_ref.at[:, 0:HALO], sem.at[0])
    bot = pltpu.make_async_copy(
        buf_ref.at[:, HALO : 2 * HALO], score_ref.at[:, SIDE - HALO : SIDE], sem.at[1]
    )
    top.start()
    bot.start()
    top.wait()
    bot.wait()


def sds(shape, dtype):
    return jax.ShapeDtypeStruct(shape, dtype)


def body(
    science, templates, cell_owner, cell_index, row_offset, col_offset, coefficients, psf_taps
):
    oy = row_offset[:, 0]
    ox = col_offset[:, 0]
    me = lax.axis_index("sky").astype(jnp.int32).reshape(1)
    info = jnp.pad(
        jnp.concatenate([cell_owner[0, :, 0], cell_index[0], oy]), (0, 128 - 78)
    ).astype(bf16)[None, :]

    packed = pl.pallas_call(
        pack_kernel,
        out_shape=sds((GROUP, PACKED, 128), bf16),
        in_specs=[VM, VM],
        out_specs=VM,
        scratch_shapes=[pltpu.VMEM((CELLS * SIDE, 128), f32)],
        name="pack",
    )(templates, info)
    stripes = lax.all_to_all(packed, "sky", 0, 0, tiled=True)

    taps = hermite_table()
    ahead = np.zeros((8, FAR), np.float32)
    ahead[:ORDERS, :TAPS] = taps
    back = np.zeros((8, FAR), np.float32)
    for u in range(TAPS):
        back[:ORDERS, (-MAXOFF - u) % FAR] = taps[:, u]
    psf = psf_taps.astype(f32)
    zero = jnp.zeros((VISITS, FAR - TAPS), f32)
    colrow = jnp.concatenate([jnp.flip(psf[:, 1], axis=1), zero], axis=1)
    rowrow = jnp.concatenate([psf[:, 0], zero], axis=1)
    psf_rows = jnp.stack([jnp.roll(colrow, -RAD, axis=1), jnp.roll(rowrow, -RAD, axis=1)], axis=1)

    across, down, colf, rowf = pl.pallas_call(
        bands_kernel,
        grid=(VISITS,),
        in_specs=[
            SM, SM, SM,
            pl.BlockSpec((8, FAR), lambda v: (0, 0)),
            pl.BlockSpec((8, FAR), lambda v: (0, 0)),
            pl.BlockSpec((1, 2, FAR), lambda v: (v, 0, 0)),
        ],
        out_specs=[
            pl.BlockSpec((1, FAR, 768), lambda v: (v, 0, 0)),
            pl.BlockSpec((1, 384, 1152), lambda v: (v, 0, 0)),
            pl.BlockSpec((1, COLS, COLS), lambda v: (v, 0, 0)),
            pl.BlockSpec((1, SIDE, FAR), lambda v: (v, 0, 0)),
        ],
        out_shape=[
            sds((VISITS, FAR, 768), bf16),
            sds((VISITS, 384, 1152), bf16),
            sds((VISITS, COLS, COLS), bf16),
            sds((VISITS, SIDE, FAR), bf16),
        ],
        scratch_shapes=[
            pltpu.VMEM((ORDERS, 360, 128), f32),
            pltpu.VMEM((ORDERS, SIDE, FAR), f32),
            pltpu.VMEM((ORDERS, SIDE, FAR), f32),
        ],
        name="bands",
    )(oy, ox, coefficients.reshape(VISITS, 126), jnp.asarray(ahead), jnp.asarray(back), psf_rows)

    picked = pl.pallas_call(
        select_kernel,
        out_shape=sds((GROUP, PICKPAD, 128), bf16),
        in_specs=[SM, VM, VM],
        out_specs=VM,
        name="select",
    )(me, stripes, jnp.asarray(request_selector()).astype(bf16))
    rows = lax.all_to_all(picked, "sky", 0, 0, tiled=True)

    difference, score, part, top, bot = pl.pallas_call(
        model_kernel,
        grid=(VISITS,),
        in_specs=[
            pl.BlockSpec((GROUP, PICKPAD, 128), lambda v: (0, 0, 0)),
            pl.BlockSpec((1, FAR, 768), lambda v: (v, 0, 0)),
            pl.BlockSpec((1, 384, 1152), lambda v: (v, 0, 0)),
            pl.BlockSpec((1, COLS, COLS), lambda v: (v, 0, 0)),
            pl.BlockSpec((1, SIDE, FAR), lambda v: (v, 0, 0)),
            pl.BlockSpec((1, SIDE, COLS), lambda v: (v, 0, 0)),
        ],
        out_specs=[
            pl.BlockSpec((1, SIDE, COLS), lambda v: (v, 0, 0)),
            pl.BlockSpec((1, SIDE, COLS), lambda v: (v, 0, 0)),
            pl.BlockSpec((1, 2 * HALO, COLS), lambda v: (v, 0, 0)),
            pl.BlockSpec((1, HALO, COLS), lambda v: (v, 0, 0)),
            pl.BlockSpec((1, HALO, COLS), lambda v: (v, 0, 0)),
        ],
        out_shape=[
            sds((VISITS, SIDE, COLS), bf16),
            sds((VISITS, SIDE, COLS), f32),
            sds((VISITS, 2 * HALO, COLS), f32),
            sds((VISITS, HALO, COLS), bf16),
            sds((VISITS, HALO, COLS), bf16),
        ],
        scratch_shapes=[
            pltpu.VMEM((GROUP * PICKPAD, 128), f32),
            pltpu.VMEM((VISITS, 192, 384), bf16),
            pltpu.VMEM((1152, COLS), bf16),
        ],
        name="model",
    )(rows, across, down, colf, rowf, science)

    count = lax.axis_size("ccd")
    above = lax.ppermute(bot, "ccd", [(i, i + 1) for i in range(count - 1)])
    below = lax.ppermute(top, "ccd", [(i + 1, i) for i in range(count - 1)])
    score = pl.pallas_call(
        edge_kernel,
        out_shape=sds((VISITS, SIDE, COLS), f32),
        in_specs=[VM, VM, VM, VM, pl.BlockSpec(memory_space=pl.ANY)],
        out_specs=pl.BlockSpec(memory_space=pl.ANY),
        scratch_shapes=[pltpu.VMEM((VISITS, 2 * HALO, COLS), f32), pltpu.SemaphoreType.DMA((2,))],
        input_output_aliases={4: 0},
        name="edges",
    )(part, above, below, rowf, score)
    return difference, score


def solution(mesh):
    in_specs = (
        P("sky", "ccd", None),
        P("sky", "ccd", None),
        P("sky", "ccd", None),
        P("sky", "ccd"),
        P("sky", "ccd"),
        P("sky", "ccd"),
        P("sky", "ccd", None, None),
        P("sky", None, None),
    )
    out_specs = (P("sky", "ccd", None), P("sky", "ccd", None))
    return jax.shard_map(body, mesh=mesh, in_specs=in_specs, out_specs=out_specs, check_vma=False)
```

time: 221 us -> 113 us (0.51)
  the two profiles are of different devices: /device:TPU:11 before, /device:TPU:22 now
where the time goes in v1:
time: 113 us
  waiting for transfers between devices  38.2 us (34%)
  Pallas kernels  35.7 us (32%)
  starting transfers between devices  30.9 us (27%)
  local copies, waits for them, and re-layouts  3.7 us (3%)
  other arithmetic  3.35 us (3%)
    all_to_all x1, waiting for transfers between devices, body(): stripes = lax.all_to_all(packed, 'sky', 0, 0, tiled=True)  23.8 us
    all_to_all x1, starting transfers between devices, body(): stripes = lax.all_to_all(packed, 'sky', 0, 0, tiled=True)  16.5 us
    pallas_call x1, Pallas kernels, body(): pl.pallas_call(bands_kernel, grid=(VISITS,), in_specs=[SM, SM, SM, pl.Blo...  14.9 us
    all_to_all x1, waiting for transfers between devices, body(): rows = lax.all_to_all(picked, 'sky', 0, 0, tiled=True)  10.4 us
    pallas_call x1, Pallas kernels, body(): pl.pallas_call(model_kernel, grid=(VISITS,), in_specs=[pl.BlockSpec((GROU...  10.2 us
    ppermute x1, starting transfers between devices, body(): above = lax.ppermute(bot, 'ccd', [(i, i + 1) for i in range(count - 1)])  6.66 us
    pallas_call x1, Pallas kernels, body(): pl.pallas_call(select_kernel, out_shape=sds((GROUP, PICKPAD, 128), bf16),...  5.94 us
    all_to_all x1, starting transfers between devices, body(): rows = lax.all_to_all(picked, 'sky', 0, 0, tiled=True)  5.65 us
  transfers between devices with their start and end apart: 4, of which 4 were waited for; matrix products, arithmetic and copies ran while one was open for 2% of the time, Pallas kernels for 13%

profile of v1, /device:TPU:22, one launch (start us, length us, event | category | flops | bytes accessed | tf_op | source)
XLA Modules:
  0.0 112.6 jit_solution(5327164791600689279)
XLA Ops:
  0.6 0.0 copy-start.5
  0.6 0.0 copy-start.4
  0.7 0.7 convert_bitcast_fusion.1
  1.3 0.7 convert_bitcast_fusion
  2.0 0.7 bitcast_convert_fusion
  2.6 0.6 fusion.info_ref
  3.2 2.6 %pack.1 = bf16[64,40,128]{2,1,0:T(8,128)(2,1)} custom-call(bf16[16,128,128]{2,1,0:T(8,128)(2,1)} %cells_ref.1, bf16[1,128]{1,0:T(2,128)(2,1)} %fusion.info_ref), custom_call_target="tpu_custom_call" | custom-call | tf_op jit(solution)/shard_map/pack/pallas_call | solution.py:246
  5.8 16.5 %all-to-all-start = ((bf16[64,40,128]{2,1,0:T(8,128)(2,1)}), bf16[64,40,128]{2,1,0:T(8,128)(2,1)S(1)}, u32[]{:S(2)}, u32[]{:S(2)}) async-start(bf16[64,40,128]{2,1,0:T(8,128)(2,1)} %pack.1), calls=%async_computation | async-start | bytes 1310720 | tf_op jit(solution)/shard_map/all_to_all | solution.py:254
  22.3 23.8 %all-to-all-done.stripes_ref = bf16[64,40,128]{2,1,0:T(8,128)(2,1)S(1)} async-done(((bf16[64,40,128]{2,1,0:T(8,128)(2,1)}), bf16[64,40,128]{2,1,0:T(8,128)(2,1)S(1)}, u32[]{:S(2)}, u32[]{:S(2)}) %all-to-all-start) | async-done | bytes 655392 | tf_op jit(solution)/shard_map/all_to_all | solution.py:254
  46.2 0.8 copy-done.1
  47.0 5.9 %select.16 = bf16[64,56,128]{2,1,0:T(8,128)(2,1)} custom-call(s32[1]{0:T(128)} %bitcast.me_ref, bf16[64,40,128]{2,1,0:T(8,128)(2,1)} %copy-done.1, bf16[168,128]{1,0:T(8,128)(2,1)} %constant.34.sel_ref), custom_call_target="tpu_custom_call" | custom-call | tf_op jit(solution)/shard_map/select/pallas_call | solution.py:297
  52.9 5.6 %all-to-all-start.1 = ((bf16[64,56,128]{2,1,0:T(8,128)(2,1)}), bf16[64,56,128]{2,1,0:T(8,128)(2,1)S(1)}, u32[]{:S(2)}, u32[]{:S(2)}) async-start(bf16[64,56,128]{2,1,0:T(8,128)(2,1)} %select.16), calls=%async_computation.1 | async-start | bytes 1835008 | tf_op jit(solution)/shard_map/all_to_all | solution.py:304
  58.6 0.1 slice.27
  58.7 0.1 rev.4
  58.8 0.1 slice.28
  58.8 0.1 pad_slice_fusion.1
  58.9 0.1 maximum_bitcast_fusion
  59.0 0.1 pad_slice_fusion
  59.1 0.1 pad_maximum_fusion.1
  59.2 0.1 copy.17
  59.3 0.7 reshape.11.coef_ref
  60.0 0.6 pad_maximum_fusion.psf_ref
  60.6 14.9 %bands.1 = (bf16[6,256,768]{2,1,0:T(8,128)(2,1)}, bf16[6,384,1152]{2,1,0:T(8,128)(2,1)}, bf16[6,256,256]{2,1,0:T(8,128)(2,1)}, bf16[6,128,256]{2,1,0:T(8,128)(2,1)}) custom-call(s32[6]{0:T(128)} %bitcast.20, s32[6]{0:T(128)} %bitcast.21, f32[6,126]{1,0:T(8,128)} %reshape.11.coef_ref, f32[8,256]{1,0:T(8,128)} %constant.17.clone.taps_ref, ...), custom_call_target="tpu_custom_call" | custom-call | tf_op jit(solution)/shard_map/bands/pallas_call | solution.py:268
  75.5 10.4 %all-to-all-done.1.rows_ref = bf16[64,56,128]{2,1,0:T(8,128)(2,1)S(1)} async-done(((bf16[64,56,128]{2,1,0:T(8,128)(2,1)}), bf16[64,56,128]{2,1,0:T(8,128)(2,1)S(1)}, u32[]{:S(2)}, u32[]{:S(2)}) %all-to-all-start.1) | async-done | bytes 917536 | tf_op jit(solution)/shard_map/all_to_all | solution.py:304
  85.9 1.0 copy-done
  86.9 10.2 %model.1 = (bf16[6,128,256]{2,1,0:T(8,128)(2,1)}, f32[6,128,256]{2,1,0:T(8,128)}, f32[6,32,256]{2,1,0:T(8,128)}, bf16[6,16,256]{2,1,0:T(8,128)(2,1)}, bf16[6,16,256]{2,1,0:T(8,128)(2,1)}) custom-call(bf16[64,56,128]{2,1,0:T(8,128)(2,1)} %copy-done, bf16[6,256,768]{2,1,0:T(8,128)(2,1)} %get-tuple-element.11.across_ref, ...), custom_call_target="tpu_custom_call" | custom-call | tf_op jit(solution)/shard_map/model/pallas_call | solution.py:306
  97.1 6.7 %collective-permute-start = (bf16[6,16,256]{2,1,0:T(8,128)(2,1)}, bf16[6,16,256]{2,1,0:T(8,128)(2,1)S(1)}, u32[]{:S(2)}, u32[]{:S(2)}) collective-permute-start(bf16[6,16,256]{2,1,0:T(8,128)(2,1)} %get-tuple-element.17), channel_id=1, source_target_pairs={{0,1},{1,2},{2,3},{3,4},{4,5},{5,6},{6,7},{8,9},{9,10},{10,11},{11... | collective-permute-start | bytes 147464 | tf_op jit(solution)/shard_map/ppermute | solution.py:340
  103.8 2.2 %collective-permute-start.1 = (bf16[6,16,256]{2,1,0:T(8,128)(2,1)}, bf16[6,16,256]{2,1,0:T(8,128)(2,1)S(1)}, u32[]{:S(2)}, u32[]{:S(2)}) collective-permute-start(bf16[6,16,256]{2,1,0:T(8,128)(2,1)} %get-tuple-element.18), channel_id=1, source_target_pairs={{1,0},{2,1},{3,2},{4,3},{5,4},{6,5},{7,6},{9,8},{10,9},{11,10},{12... | collective-permute-start | bytes 147464 | tf_op jit(solution)/shard_map/ppermute | solution.py:341
  106.0 0.3 collective-permute-done.above_ref
  106.3 3.7 %collective-permute-done.1.below_ref = bf16[6,16,256]{2,1,0:T(8,128)(2,1)S(1)} collective-permute-done((bf16[6,16,256]{2,1,0:T(8,128)(2,1)}, bf16[6,16,256]{2,1,0:T(8,128)(2,1)S(1)}, u32[]{:S(2)}, u32[]{:S(2)}) %collective-permute-start.1) | collective-permute-done | bytes 49184 | tf_op jit(solution)/shard_map/ppermute | solution.py:341
  110.0 0.6 copy-done.3
  110.6 2.0 %edges.1 = f32[6,128,256]{2,1,0:T(8,128)} custom-call(f32[6,32,256]{2,1,0:T(8,128)} %get-tuple-element.16.part_ref, bf16[6,16,256]{2,1,0:T(8,128)(2,1)} %copy-done.2, bf16[6,16,256]{2,1,0:T(8,128)(2,1)} %copy-done.3, bf16[6,128,256]{2,1,0:T(8,128)(2,1)} %get-tuple-element.14.rowf_ref, f32[6,128,256]{2,1,0:T(8,128)} %get-tuple-element.19._), custom_call_target="tpu_custom_call", output_to_operand_aliasing={{}: (4, {})} | custom-call | tf_op jit(solution)/shard_map/edges/pallas_call | solution.py:342
  (11 shorter events, 0.0 us)
Async XLA Ops:
  0.6 58.0 %copy-start.5 = (bf16[6,2,31]{2,1,0:T(2,128)(2,1)S(1)}, bf16[6,2,31]{2,1,0:T(2,128)(2,1)}, u32[]{:S(2)}) copy-start(bf16[6,2,31]{2,1,0:T(2,128)(2,1)} %param.18) | copy-start | bytes 2236
  0.6 58.5 %copy-start.4 = (f32[6,1,21,6]{2,1,3,0:T(1,128)S(1)}, f32[6,1,21,6]{2,1,3,0:T(1,128)}, u32[]{:S(2)}) copy-start(f32[6,1,21,6]{2,1,3,0:T(1,128)} %param.17) | copy-start | bytes 9076
  5.8 40.3 %all-to-all-start = ((bf16[64,40,128]{2,1,0:T(8,128)(2,1)}), bf16[64,40,128]{2,1,0:T(8,128)(2,1)S(1)}, u32[]{:S(2)}, u32[]{:S(2)}) async-start(bf16[64,40,128]{2,1,0:T(8,128)(2,1)} %pack.1), calls=%async_computation | async-start | bytes 1310720 | tf_op jit(solution)/shard_map/all_to_all | solution.py:254
  46.2 0.8 copy-start.1
  52.9 32.9 %all-to-all-start.1 = ((bf16[64,56,128]{2,1,0:T(8,128)(2,1)}), bf16[64,56,128]{2,1,0:T(8,128)(2,1)S(1)}, u32[]{:S(2)}, u32[]{:S(2)}) async-start(bf16[64,56,128]{2,1,0:T(8,128)(2,1)} %select.16), calls=%async_computation.1 | async-start | bytes 1835008 | tf_op jit(solution)/shard_map/all_to_all | solution.py:304
  85.9 1.0 copy-start
  97.1 9.2 %collective-permute-start = (bf16[6,16,256]{2,1,0:T(8,128)(2,1)}, bf16[6,16,256]{2,1,0:T(8,128)(2,1)S(1)}, u32[]{:S(2)}, u32[]{:S(2)}) collective-permute-start(bf16[6,16,256]{2,1,0:T(8,128)(2,1)} %get-tuple-element.17), channel_id=1, source_target_pairs={{0,1},{1,2},{2,3},{3,4},{4,5},{5,6},{6,7},{8,9},{9,10},{10,11},{11... | collective-permute-start | bytes 147464 | tf_op jit(solution)/shard_map/ppermute | solution.py:340
  103.8 6.2 %collective-permute-start.1 = (bf16[6,16,256]{2,1,0:T(8,128)(2,1)}, bf16[6,16,256]{2,1,0:T(8,128)(2,1)S(1)}, u32[]{:S(2)}, u32[]{:S(2)}) collective-permute-start(bf16[6,16,256]{2,1,0:T(8,128)(2,1)} %get-tuple-element.18), channel_id=1, source_target_pairs={{1,0},{2,1},{3,2},{4,3},{5,4},{6,5},{7,6},{9,8},{10,9},{11,10},{12... | collective-permute-start | bytes 147464 | tf_op jit(solution)/shard_map/ppermute | solution.py:341
  106.3 3.7 %copy-start.2 = (bf16[6,16,256]{2,1,0:T(8,128)(2,1)}, bf16[6,16,256]{2,1,0:T(8,128)(2,1)S(1)}, u32[]{:S(2)}) copy-start(bf16[6,16,256]{2,1,0:T(8,128)(2,1)S(1)} %collective-permute-done.above_ref) | copy-start | bytes 147460
  110.0 0.6 copy-start.3

commit v2 on v1

v2 whole, which is shorter than its diff:
```python
import jax
import jax.numpy as jnp
import numpy as np
from jax import lax
from jax.experimental import pallas as pl
from jax.experimental.pallas import tpu as pltpu
from jax.sharding import PartitionSpec as P

RAD = 15
TAPS = 31
ORDERS = 6
GROUP = 64
CELLS = 16
SIDE = 128
VISITS = 6
COLS = 256
HALO = 16
STRIPE = 32
PACKED = 40
PICKS = 40
LONG = 1024
MAXOFF = 98
FAR = 256
f32 = jnp.float32
bf16 = jnp.bfloat16
VM = pl.BlockSpec(memory_space=pltpu.VMEM)
HB = pl.BlockSpec(memory_space=pltpu.HBM)
SM = pl.BlockSpec(memory_space=pltpu.SMEM)
LIMIT = pltpu.CompilerParams(vmem_limit_bytes=32 * 2**20)


def hermite_table():
    t = (np.arange(TAPS, dtype=np.float32) - np.float32(RAD)) / np.float32(4.0)
    series = [np.ones(t.shape, np.float32), np.float32(2.0) * t]
    for n in range(1, ORDERS - 1):
        series.append(np.float32(2.0) * t * series[n] - np.float32(2.0 * n) * series[n - 1])
    w = np.stack(series) * np.exp(np.float32(-0.5) * t * t)
    w = w / np.sqrt(np.sum(w * w, axis=1, keepdims=True))
    return np.asarray(w, dtype=jnp.bfloat16).astype(np.float32)


def quarter(x, k):
    return pltpu.roll(x, (k % 4) * 32, 1) if k % 4 else x


def choose(quarters, *items):
    out = items[-1]
    for mask, item in zip(quarters, items[:-1]):
        out = jnp.where(mask, item, out)
    return out


def quarter_masks(count):
    at = lax.broadcasted_iota(jnp.int32, (count, 128), 1) // 32
    return [at == k for k in range(3)]


def transpose_quarters(items, masks):
    turned = [quarter(x, j) for j, x in enumerate(items)]
    return [
        quarter(choose(masks, *(turned[(m - t) % 4] for m in range(4))), -t) for t in range(4)
    ]


def across_band(taps):
    band = np.zeros((FAR, ORDERS * 128), np.float32)
    for i in range(ORDERS):
        for x in range(128):
            band[x : x + TAPS, i * 128 + x] = taps[i]
    return band


def scatter_rows():
    r = lax.broadcasted_iota(jnp.int32, (256, 256), 0)
    c = lax.broadcasted_iota(jnp.int32, (256, 256), 1)
    return jnp.where(c == (r % 8) * 32 + r // 8, 1.0, 0.0).astype(bf16)


def gather_rows():
    r = lax.broadcasted_iota(jnp.int32, (256, 256), 0)
    c = lax.broadcasted_iota(jnp.int32, (256, 256), 1)
    source = ((r % 16) * 2 + (r // 16) % 2) * 8 + r // 32
    return jnp.where(c == source, 1.0, 0.0).astype(bf16)


def pack_kernel(
    cells_any, owner_any, index_any, oy_any, ox_any, out_ref,
    cells_ref, owner_ref, index_ref, oy_ref, ox_ref, info_ref, sem,
):
    copies = [
        pltpu.make_async_copy(src, dst, sem.at[k])
        for k, (src, dst) in enumerate(
            (
                (cells_any, cells_ref), (owner_any, owner_ref), (index_any, index_ref),
                (oy_any, oy_ref), (ox_any, ox_ref),
            )
        )
    ]
    for copy in copies:
        copy.start()
    move = scatter_rows()
    masks = quarter_masks(256)
    info_ref[...] = jnp.zeros((8, 128), f32)
    for copy in copies[1:]:
        copy.wait()
    info_ref[0:1, 0:36] = owner_ref[...].astype(f32)
    info_ref[1:2, 0:36] = index_ref[...].astype(f32)
    info_ref[2:3, 0:VISITS] = oy_ref[...].astype(f32)
    info_ref[3:4, 0:VISITS] = ox_ref[...].astype(f32)
    info = info_ref[...].astype(bf16)
    for d in range(GROUP):
        out_ref[d // 2, d % 2, STRIPE:PACKED, :] = info
    copies[0].wait()
    moved = []
    for q in range(4):
        halves = [
            cells_ref[h * 8 : (h + 1) * 8, q * 32 : (q + 1) * 32, :].reshape(256, 128)
            for h in range(2)
        ]
        moved.append(
            jnp.dot(move, jnp.concatenate(halves, axis=1), preferred_element_type=f32)
        )
    for h in range(2):
        groups = transpose_quarters([m[:, h * 128 : (h + 1) * 128] for m in moved], masks)
        for c in range(2):
            for u in range(2):
                at = u * CELLS + h * 8
                out_ref[:, c, at : at + 8, :] = groups[c + 2 * u].reshape(32, 8, 128).astype(bf16)


def select_kernel(me_ref, stripes_ref, out_ref, asks_ref):
    table = jnp.concatenate(
        [
            stripes_ref[:, 0:CELLS, :].reshape(GROUP * CELLS, 128),
            stripes_ref[:, CELLS:STRIPE, :].reshape(GROUP * CELLS, 128),
        ],
        axis=1,
    )
    me = me_ref[0]
    own = (me // 2).astype(f32)
    core = (me % 2).astype(f32)
    for n in range(GROUP):
        asks_ref[:, n, :] = stripes_ref[n, STRIPE:PACKED, :].astype(f32)
    ids = asks_ref[0] * CELLS + asks_ref[1]
    tops = asks_ref[2]
    lefts = asks_ref[3]
    lane = lax.broadcasted_iota(jnp.int32, (GROUP, 128), 1)
    number = [(lane + 128 * k).astype(f32) for k in range(GROUP * CELLS // 128)]
    first = (lane // 32 * 32).astype(f32) + own
    masks = quarter_masks(GROUP)
    move = scatter_rows()

    def column(x, k):
        return jnp.broadcast_to(x[:, k : k + 1], (GROUP, 128))

    lines, last = [], []
    fifths = []
    for v in range(VISITS):
        hot = []
        for r in range(6):
            want = column(ids, v * 6 + r)
            hot.append(
                jnp.concatenate(
                    [jnp.where(n == want, 1.0, 0.0).astype(bf16) for n in number], axis=1
                )
            )
        got = jnp.dot(jnp.concatenate(hot, axis=0), table, preferred_element_type=f32)
        above = first >= column(tops, v)
        late = column(lefts, v) >= 32.0 * (core + 1.0)
        whole, fifth = [], []
        for b in range(3):
            for u in range(2):
                upper = got[b * GROUP : (b + 1) * GROUP, u * 128 : (u + 1) * 128]
                lower = got[(3 + b) * GROUP : (4 + b) * GROUP, u * 128 : (u + 1) * 128]
                whole.append(jnp.where(above, upper, quarter(lower, -1)))
                fifth.append(lower)
        whole[0] = jnp.where(late, whole[5], whole[0])
        fifth[0] = jnp.where(late, fifth[5], fifth[0])
        lines += [w.astype(bf16) for w in whole[:5]]
        fifths.append(choose(masks, *(quarter(fifth[k], k) for k in range(4))).astype(bf16))
        last.append(quarter(fifth[4], v))
    lines += fifths
    lines.append(choose(masks, *last[:4]).astype(bf16))
    lines.append(choose(masks, last[4], last[5], last[5], last[5]).astype(bf16))
    lines += [lines[-1], lines[-1]]
    for k in range(PICKS // 8):
        block = jnp.concatenate(
            [
                jnp.concatenate([x[h * 32 : (h + 1) * 32] for x in lines[k * 8 : k * 8 + 8]], axis=0)
                for h in range(2)
            ],
            axis=1,
        )
        moved = jnp.dot(move, block, preferred_element_type=f32)
        for h in range(2):
            out_ref[h * 32 : (h + 1) * 32, k * 8 : k * 8 + 8, :] = (
                moved[:, h * 128 : (h + 1) * 128].reshape(32, 8, 128).astype(bf16)
            )


def bands_kernel(
    oy_ref, coef_ref, taps_ref, psf_ref, down_ref, colf_ref, rowf_ref, toep_ref, shift_ref,
):
    v = pl.program_id(0)

    def spread(row, count):
        return pltpu.roll(jnp.broadcast_to(row, (count, FAR)), 0, 1, stride=1, stride_axis=0)

    @pl.when(v == 0)
    def _():
        for i in range(ORDERS):
            toep_ref[i] = spread(taps_ref[i : i + 1, :], SIDE)

    oy = oy_ref[v]
    for i in range(ORDERS):
        shift_ref[i] = pltpu.roll(toep_ref[i], oy, 1)
    near = lax.broadcasted_iota(jnp.int32, (COLS, COLS), 0) - lax.broadcasted_iota(
        jnp.int32, (COLS, COLS), 1
    )
    colf_ref[0] = jnp.where(
        jnp.abs(near) <= RAD, spread(psf_ref[0, 0:1, :], COLS), 0.0
    ).astype(bf16)
    rowf_ref[0] = spread(psf_ref[0, 1:2, :], SIDE).astype(bf16)

    masks = quarter_masks(16)
    three = lax.broadcasted_iota(jnp.int32, (16, 128), 1) < 96

    def step(g, _):
        row = lax.broadcasted_iota(jnp.int32, (16, 128), 0) + g * 16
        ty = (2.0 * row.astype(f32) + 1.0) / SIDE - 1.0
        bands = [shift_ref[j, pl.ds(g * 16, 16), :] for j in range(ORDERS)]
        first = 0
        fifth = []
        for i in range(ORDERS):
            sums = [None] * 6
            for j in range(ORDERS - i):
                c = [coef_ref[v, (first + j) * 6 + p] for p in range(6)]
                flat = c[0] + ty * (c[2] + ty * c[5])
                slope = c[1] + ty * c[4]
                for part in range(2):
                    band = bands[j][:, part * 128 : (part + 1) * 128]
                    for q, weight in enumerate((flat, slope, c[3])):
                        term = weight * band
                        at = q * 2 + part
                        sums[at] = term if sums[at] is None else sums[at] + term
            first += ORDERS - i
            ends = []
            for q in range(3):
                low, high = sums[q * 2], sums[q * 2 + 1]
                down_ref[0, pl.ds(q * SIDE + g * 16, 16), i * 128 : (i + 1) * 128] = (
                    low + jnp.where(three, quarter(high, -1), 0.0)
                ).astype(bf16)
                ends.append(quarter(high, i))
            fifth.append(ends)
        for q in range(3):
            row_at = pl.ds(q * SIDE + g * 16, 16)
            down_ref[0, row_at, 768:896] = choose(masks, *(fifth[i][q] for i in range(4))).astype(
                bf16
            )
            gap = jnp.zeros((16, 128), f32)
            down_ref[0, row_at, 896:1024] = choose(
                masks, fifth[4][q], fifth[5][q], gap, gap
            ).astype(bf16)
        return 0

    lax.fori_loop(0, SIDE // 16, step, 0)


def model_kernel(
    ox_ref, rows_ref, across_any, down_any, colf_any, rowf_any, sci_any,
    diff_any, score_any, part_ref, top_ref, bot_ref,
    across_ref, down_ref, colf_ref, rowf_ref, sci_ref, diff_ref, score_ref,
    win_ref, stack_ref, sem, out_sem,
):
    band = pltpu.make_async_copy(across_any, across_ref, sem.at[VISITS, 0])
    band.start()
    fetch = [
        [
            pltpu.make_async_copy(src.at[v], dst.at[v], sem.at[v, k])
            for k, (src, dst) in enumerate(
                ((down_any, down_ref), (colf_any, colf_ref), (rowf_any, rowf_ref), (sci_any, sci_ref))
            )
        ]
        for v in range(VISITS)
    ]
    for copies in fetch:
        for copy in copies:
            copy.start()
    half = GROUP // 2
    move = gather_rows()
    masks = quarter_masks(half)
    lane = lax.broadcasted_iota(jnp.int32, (160, 128), 1)
    lines = []
    for k in range(PICKS // 8):
        block = jnp.concatenate(
            [
                rows_ref[h * 32 : (h + 1) * 32, k * 8 : k * 8 + 8, :].reshape(256, 128)
                for h in range(2)
            ],
            axis=1,
        )
        lines.append(jnp.dot(move, block, preferred_element_type=f32))

    def take(row, c):
        at = (row % 8) * 32 + c * 16
        return jnp.concatenate(
            [lines[row // 8][at : at + 16, h * 128 : (h + 1) * 128] for h in range(2)], axis=0
        )

    def window(v):
        groups = [[take(v * 5 + k, c) for c in range(2)] for k in range(5)]
        blocks = [
            transpose_quarters(
                [groups[k][0], groups[k][1], groups[m][0], groups[m][1]], masks
            )
            for k, m in ((0, 1), (2, 3), (4, 0))
        ]
        e = [take(30 + v, c) for c in range(2)]
        f = [take(36 + v // 4, c) for c in range(2)]
        fifths = [
            choose(masks, e[0], quarter(e[1], 1), quarter(e[0], 1), quarter(e[1], 2)),
            choose(masks, quarter(e[0], 2), quarter(e[1], 3), quarter(e[0], 3), e[1]),
            choose(
                masks, quarter(f[0], -v), quarter(f[1], 1 - v), quarter(e[0], 2), quarter(e[1], 3)
            ),
        ]
        back = 128 - ox_ref[v]
        turned = [
            pltpu.roll(jnp.concatenate(blocks[b] + [fifths[b]], axis=0), back, 1)
            for b in range(3)
        ]
        tiles = [
            jnp.where(lane < back, turned[b], turned[min(b + 1, 2)]).astype(bf16) for b in range(3)
        ]
        for xb in range(2):
            at = v * 320 + xb * 160
            win_ref[at : at + 160, 0:128] = tiles[xb]
            win_ref[at : at + 160, 128:256] = tiles[xb + 1]

    col = lax.broadcasted_iota(jnp.int32, (SIDE, COLS), 1).astype(f32)
    tx = (2.0 * col + 1.0) / COLS - 1.0
    out = []

    def spread(group):
        at = group[0] * 320
        got = jnp.dot(
            win_ref[at : at + 320 * len(group), :], across_ref[...], preferred_element_type=f32
        ).astype(bf16)
        for n, v in enumerate(group):
            stack_ref[v, 960:LONG, :] = jnp.zeros((LONG - 960, COLS), bf16)
            for xb in range(2):
                row = n * 320 + xb * 160
                for i in range(ORDERS):
                    piece = got[row : row + 160, i * 128 : (i + 1) * 128]
                    low = ORDERS * 128 + i * half
                    cols = slice(xb * 128, (xb + 1) * 128)
                    stack_ref[v, i * 128 : (i + 1) * 128, cols] = piece[0:128]
                    stack_ref[v, low : low + half, cols] = piece[128:160]

    def finish(v):
        parts = jnp.dot(down_ref[v], stack_ref[v], preferred_element_type=f32)
        model = parts[0:128] + tx * (parts[128:256] + tx * parts[256:384])
        diff = (sci_ref[v].astype(f32) - model).astype(bf16)
        diff_ref[v] = diff
        filt = jnp.dot(diff, colf_ref[v], preferred_element_type=f32).astype(bf16)
        top_ref[v] = filt[0:HALO]
        bot_ref[v] = filt[SIDE - HALO :]
        score = jnp.dot(rowf_ref[v, :, 0:128], filt, preferred_element_type=f32)
        score_ref[v] = score
        part_ref[v, 0:HALO] = score[0:HALO]
        part_ref[v, HALO:] = score[SIDE - HALO :]
        out.append(pltpu.make_async_copy(diff_ref.at[v], diff_any.at[v], out_sem.at[v, 0]))
        out.append(pltpu.make_async_copy(score_ref.at[v], score_any.at[v], out_sem.at[v, 1]))
        out[-2].start()
        out[-1].start()

    early, rest = (0, 1, 2), (3, 4, 5)
    for v in early:
        window(v)
    band.wait()
    spread(early)
    for v in rest:
        window(v)
    for v in early:
        for copy in fetch[v]:
            copy.wait()
    spread(rest)
    for v in early:
        finish(v)
    for v in rest:
        for copy in fetch[v]:
            copy.wait()
    for v in rest:
        finish(v)
    for copy in out:
        copy.wait()


def edge_kernel(part_ref, above_ref, below_ref, rowf_ref, _, score_ref, buf_ref, sem):
    for v in range(VISITS):
        gap = jnp.zeros((128 - 2 * HALO, COLS), bf16)
        ring = jnp.concatenate([below_ref[v], gap, above_ref[v]], axis=0)
        band = jnp.concatenate(
            [rowf_ref[v, 0:HALO, 128:256], rowf_ref[v, SIDE - HALO :, 128:256]], axis=0
        )
        buf_ref[v] = part_ref[v] + jnp.dot(band, ring, preferred_element_type=f32)
    top = pltpu.make_async_copy(buf_ref.at[:, 0:HALO], score_ref.at[:, 0:HALO], sem.at[0])
    bot = pltpu.make_async_copy(
        buf_ref.at[:, HALO : 2 * HALO], score_ref.at[:, SIDE - HALO : SIDE], sem.at[1]
    )
    top.start()
    bot.start()
    top.wait()
    bot.wait()


def sds(shape, dtype):
    return jax.ShapeDtypeStruct(shape, dtype)


def near(x):
    return pltpu.with_memory_space_constraint(x, pltpu.VMEM)


def body(
    science, templates, cell_owner, cell_index, row_offset, col_offset, coefficients, psf_taps
):
    oy = row_offset[:, 0]
    ox = col_offset[:, 0]
    me = lax.axis_index("sky").astype(jnp.int32).reshape(1)

    packed = pl.pallas_call(
        pack_kernel,
        out_shape=sds((GROUP // 2, 2, PACKED, 128), bf16),
        in_specs=[HB] * 5,
        out_specs=VM,
        scratch_shapes=[
            pltpu.VMEM((CELLS, SIDE, 128), bf16),
            pltpu.VMEM((1, 36), jnp.int32),
            pltpu.VMEM((1, 36), jnp.int32),
            pltpu.VMEM((1, VISITS), jnp.int32),
            pltpu.VMEM((1, VISITS), jnp.int32),
            pltpu.VMEM((8, 128), f32),
            pltpu.SemaphoreType.DMA((5,)),
        ],
        name="pack",
    )(templates, cell_owner.reshape(1, 36), cell_index, oy.reshape(1, 6), ox.reshape(1, 6))
    stripes = lax.all_to_all(packed.reshape(GROUP, PACKED, 128), "sky", 0, 0, tiled=True)

    taps = hermite_table()
    ahead = np.zeros((8, FAR), np.float32)
    ahead[:ORDERS, :TAPS] = taps
    psf = psf_taps.astype(f32)
    zero = jnp.zeros((VISITS, FAR - TAPS), f32)
    colrow = jnp.concatenate([jnp.flip(psf[:, 1], axis=1), zero], axis=1)
    rowrow = jnp.concatenate([psf[:, 0], zero], axis=1)
    psf_rows = jnp.stack([jnp.roll(colrow, -RAD, axis=1), jnp.roll(rowrow, -RAD, axis=1)], axis=1)

    down, colf, rowf = pl.pallas_call(
        bands_kernel,
        grid=(VISITS,),
        in_specs=[
            SM, SM,
            pl.BlockSpec((8, FAR), lambda v: (0, 0)),
            pl.BlockSpec((1, 2, FAR), lambda v: (v, 0, 0)),
        ],
        out_specs=[
            pl.BlockSpec((1, 384, LONG), lambda v: (v, 0, 0)),
            pl.BlockSpec((1, COLS, COLS), lambda v: (v, 0, 0)),
            pl.BlockSpec((1, SIDE, FAR), lambda v: (v, 0, 0)),
        ],
        out_shape=[
            sds((VISITS, 384, LONG), bf16),
            sds((VISITS, COLS, COLS), bf16),
            sds((VISITS, SIDE, FAR), bf16),
        ],
        scratch_shapes=[
            pltpu.VMEM((ORDERS, SIDE, FAR), f32),
            pltpu.VMEM((ORDERS, SIDE, FAR), f32),
        ],
        name="bands",
    )(oy, coefficients.reshape(VISITS, 126), jnp.asarray(ahead), psf_rows)
    stripes, down = lax.optimization_barrier((stripes, down))

    picked = pl.pallas_call(
        select_kernel,
        out_shape=sds((GROUP, PICKS, 128), bf16),
        in_specs=[SM, VM],
        out_specs=VM,
        scratch_shapes=[pltpu.VMEM((8, GROUP, 128), f32)],
        compiler_params=LIMIT,
        name="select",
    )(me, near(stripes))
    rows = lax.all_to_all(picked, "sky", 0, 0, tiled=True)

    difference, score, part, top, bot = pl.pallas_call(
        model_kernel,
        in_specs=[SM, VM] + [HB] * 5,
        out_specs=[HB, HB, VM, VM, VM],
        out_shape=[
            sds((VISITS, SIDE, COLS), bf16),
            sds((VISITS, SIDE, COLS), f32),
            pltpu.VMEM((VISITS, 2 * HALO, COLS), f32),
            sds((VISITS, HALO, COLS), bf16),
            sds((VISITS, HALO, COLS), bf16),
        ],
        scratch_shapes=[
            pltpu.VMEM((FAR, 768), bf16),
            pltpu.VMEM((VISITS, 384, LONG), bf16),
            pltpu.VMEM((VISITS, COLS, COLS), bf16),
            pltpu.VMEM((VISITS, SIDE, FAR), bf16),
            pltpu.VMEM((VISITS, SIDE, COLS), bf16),
            pltpu.VMEM((VISITS, SIDE, COLS), bf16),
            pltpu.VMEM((VISITS, SIDE, COLS), f32),
            pltpu.VMEM((VISITS * 320, 256), bf16),
            pltpu.VMEM((VISITS, LONG, COLS), bf16),
            pltpu.SemaphoreType.DMA((VISITS + 1, 4)),
            pltpu.SemaphoreType.DMA((VISITS, 2)),
        ],
        name="model",
    )(ox, near(rows), jnp.asarray(across_band(taps)).astype(bf16), down, colf, rowf, science)

    count = lax.axis_size("ccd")
    above = lax.ppermute(bot, "ccd", [(i, i + 1) for i in range(count - 1)])
    below = lax.ppermute(top, "ccd", [(i + 1, i) for i in range(count - 1)])
    score = pl.pallas_call(
        edge_kernel,
        out_shape=sds((VISITS, SIDE, COLS), f32),
        in_specs=[VM, VM, VM, VM, pl.BlockSpec(memory_space=pl.ANY)],
        out_specs=pl.BlockSpec(memory_space=pl.ANY),
        scratch_shapes=[pltpu.VMEM((VISITS, 2 * HALO, COLS), f32), pltpu.SemaphoreType.DMA((2,))],
        input_output_aliases={4: 0},
        compiler_params=LIMIT,
        name="edges",
    )(part, near(above), near(below), rowf, score)
    return difference, score


def solution(mesh):
    in_specs = (
        P("sky", "ccd", None),
        P("sky", "ccd", None),
        P("sky", "ccd", None),
        P("sky", "ccd"),
        P("sky", "ccd"),
        P("sky", "ccd"),
        P("sky", "ccd", None, None),
        P("sky", None, None),
    )
    out_specs = (P("sky", "ccd", None), P("sky", "ccd", None))
    return jax.shard_map(body, mesh=mesh, in_specs=in_specs, out_specs=out_specs, check_vma=False)
```

time: 113 us -> 95.8 us (0.85)
  the two profiles are of different devices: /device:TPU:22 before, /device:TPU:24 now
where the time goes in v2:
time: 95.8 us; the launch traced here: 95.4 us
  blocking collectives  29.5 us (31%)
  Pallas kernels  28.1 us (29%)
  starting transfers between devices  25.4 us (27%)
  waiting for transfers between devices  8.38 us (9%)
  local copies, waits for them, and re-layouts  1.91 us (2%)
  other arithmetic  1.46 us (2%)
    all_to_all x1, blocking collectives, body(): rows = lax.all_to_all(picked, 'sky', 0, 0, tiled=True)  29.5 us
    all_to_all x1, starting transfers between devices, body(): lax.all_to_all(packed.reshape(GROUP, PACKED, 128), 'sky', 0, 0, tiled=True)  15.6 us
    pallas_call x1, Pallas kernels, body(): pl.pallas_call(bands_kernel, grid=(VISITS,), in_specs=[SM, SM, pl.BlockSp...  13.6 us
    pallas_call x1, Pallas kernels, body(): pl.pallas_call(model_kernel, in_specs=[SM, VM] + [HB] * 5, out_specs=[HB,...  9.03 us
    ppermute x1, starting transfers between devices, body(): above = lax.ppermute(bot, 'ccd', [(i, i + 1) for i in range(count - 1)])  7.89 us
    ppermute x1, waiting for transfers between devices, body(): below = lax.ppermute(top, 'ccd', [(i + 1, i) for i in range(count - 1)])  5.05 us
    all_to_all x1, waiting for transfers between devices, body(): lax.all_to_all(packed.reshape(GROUP, PACKED, 128), 'sky', 0, 0, tiled=True)  3.22 us
    pallas_call x1, Pallas kernels, body(): pl.pallas_call(pack_kernel, out_shape=sds((GROUP // 2, 2, PACKED, 128), b...  2.67 us
  transfers between devices with their start and end apart: 3, of which 3 were waited for; matrix products, arithmetic and copies ran while one was open for 4% of the time, Pallas kernels for 14%

profile of v2, /device:TPU:24, one launch (start us, length us, event | category | flops | bytes accessed | tf_op | source)
XLA Modules:
  0.0 95.4 jit_solution(1240292065836772056)
XLA Ops:
  0.6 2.7 %pack.1 = bf16[32,2,40,128]{3,2,1,0:T(8,128)(2,1)} custom-call(bf16[16,128,128]{2,1,0:T(8,128)(2,1)} %cells_any.1, s32[1,36]{1,0:T(1,128)} %bitcast.22, s32[1,36]{1,0:T(1,128)} %index_any.1, s32[1,6]{1,0:T(1,128)} %bitcast.18, s32[1,6]{1,0:T(1,128)} %bitcast.20), custom_call_target="tpu_custom_call" | custom-call | tf_op jit(solution)/shard_map/pack/pallas_call | solution.py:432
  3.3 15.6 %all-to-all-start = ((bf16[64,40,128]{2,1,0:T(8,128)(2,1)}), bf16[64,40,128]{2,1,0:T(8,128)(2,1)S(1)}, u32[]{:S(2)}, u32[]{:S(2)}) async-start(bf16[64,40,128]{2,1,0:T(8,128)(2,1)} %bitcast.16), calls=%async_computation | async-start | bytes 1310720 | tf_op jit(solution)/shard_map/all_to_all | solution.py:448
  18.9 0.7 copy_convert_fusion
  19.6 0.1 slice.27
  19.7 0.1 rev.4
  19.7 0.1 slice.28
  19.8 0.1 pad_slice_fusion.1
  19.9 0.1 maximum_bitcast_fusion
  20.0 0.1 pad_slice_fusion
  20.0 0.1 pad_maximum_fusion.1
  20.1 0.8 copy.16
  21.0 0.7 reshape.19.coef_ref
  21.7 0.6 pad_maximum_fusion.psf_ref
  22.3 13.6 %bands.1 = (bf16[6,384,1024]{2,1,0:T(8,128)(2,1)}, bf16[6,256,256]{2,1,0:T(8,128)(2,1)}, bf16[6,128,256]{2,1,0:T(8,128)(2,1)}) custom-call(s32[6]{0:T(128)} %bitcast.19, f32[6,126]{1,0:T(8,128)} %reshape.19.coef_ref, f32[8,256]{1,0:T(8,128)} %constant.12.clone.taps_ref, f32[6,2,256]{2,1,0:T(2,128)} %pad_maximum_fusion.psf_ref), custom_call_target="tpu_custom_call" | custom-call | tf_op jit(solution)/shard_map/bands/pallas_call | solution.py:459
  35.9 3.2 %all-to-all-done.stripes_ref = bf16[64,40,128]{2,1,0:T(8,128)(2,1)S(1)} async-done(((bf16[64,40,128]{2,1,0:T(8,128)(2,1)}), bf16[64,40,128]{2,1,0:T(8,128)(2,1)S(1)}, u32[]{:S(2)}, u32[]{:S(2)}) %all-to-all-start) | async-done | bytes 655392 | tf_op jit(solution)/shard_map/all_to_all | solution.py:448
  39.1 0.0 copy-start
  39.1 1.9 %select.3 = bf16[64,40,128]{2,1,0:T(8,128)(2,1)S(1)} custom-call(s32[1]{0:T(128)} %bitcast.1.me_ref, bf16[64,40,128]{2,1,0:T(8,128)(2,1)S(1)} %all-to-all-done.stripes_ref), custom_call_target="tpu_custom_call" | custom-call | tf_op jit(solution)/shard_map/select/pallas_call | solution.py:485
  41.0 29.5 %all_to_all.10.rows_ref = bf16[64,40,128]{2,1,0:T(8,128)(2,1)S(1)} all-to-all(bf16[64,40,128]{2,1,0:T(8,128)(2,1)S(1)} %select.3), channel_id=1, replica_groups=mesh['sky'=64,'ccd'=8] {'sky'}, dimensions={0} | all-to-all | bytes 1310720 | tf_op jit(solution)/shard_map/all_to_all | solution.py:494
  70.5 9.0 %model.1 = (bf16[6,128,256]{2,1,0:T(8,128)(2,1)}, f32[6,128,256]{2,1,0:T(8,128)}, f32[6,32,256]{2,1,0:T(8,128)S(1)}, bf16[6,16,256]{2,1,0:T(8,128)(2,1)}, bf16[6,16,256]{2,1,0:T(8,128)(2,1)}) custom-call(s32[6]{0:T(128)} %bitcast.21, bf16[64,40,128]{2,1,0:T(8,128)(2,1)S(1)} %all_to_all.10.rows_ref, bf16[256,768]{1,0:T(8,128)(2,1)} %constant.26.across_any, ...), custom_call_target="tpu_custom_call" | custom-call | tf_op jit(solution)/shard_map/model/pallas_call | solution.py:496
  79.5 7.9 %collective-permute-start = (bf16[6,16,256]{2,1,0:T(8,128)(2,1)}, bf16[6,16,256]{2,1,0:T(8,128)(2,1)S(1)}, u32[]{:S(2)}, u32[]{:S(2)}) collective-permute-start(bf16[6,16,256]{2,1,0:T(8,128)(2,1)} %get-tuple-element.19), channel_id=1, source_target_pairs={{0,1},{1,2},{2,3},{3,4},{4,5},{5,6},{6,7},{8,9},{9,10},{10,11},{11... | collective-permute-start | bytes 147464 | tf_op jit(solution)/shard_map/ppermute | solution.py:524
  87.4 1.9 %collective-permute-start.1 = (bf16[6,16,256]{2,1,0:T(8,128)(2,1)}, bf16[6,16,256]{2,1,0:T(8,128)(2,1)S(1)}, u32[]{:S(2)}, u32[]{:S(2)}) collective-permute-start(bf16[6,16,256]{2,1,0:T(8,128)(2,1)} %get-tuple-element.20), channel_id=1, source_target_pairs={{1,0},{2,1},{3,2},{4,3},{5,4},{6,5},{7,6},{9,8},{10,9},{11,10},{12... | collective-permute-start | bytes 147464 | tf_op jit(solution)/shard_map/ppermute | solution.py:525
  89.3 0.1 collective-permute-done.above_ref
  89.5 5.0 %collective-permute-done.1.below_ref = bf16[6,16,256]{2,1,0:T(8,128)(2,1)S(1)} collective-permute-done((bf16[6,16,256]{2,1,0:T(8,128)(2,1)}, bf16[6,16,256]{2,1,0:T(8,128)(2,1)S(1)}, u32[]{:S(2)}, u32[]{:S(2)}) %collective-permute-start.1) | collective-permute-done | bytes 49184 | tf_op jit(solution)/shard_map/ppermute | solution.py:525
  94.5 0.0 copy-done
  94.5 0.9 edges.1
  (3 shorter events, 0.0 us)
Async XLA Ops:
  3.3 35.8 %all-to-all-start = ((bf16[64,40,128]{2,1,0:T(8,128)(2,1)}), bf16[64,40,128]{2,1,0:T(8,128)(2,1)S(1)}, u32[]{:S(2)}, u32[]{:S(2)}) async-start(bf16[64,40,128]{2,1,0:T(8,128)(2,1)} %bitcast.16), calls=%async_computation | async-start | bytes 1310720 | tf_op jit(solution)/shard_map/all_to_all | solution.py:448
  39.1 55.4 %copy-start = (bf16[6,128,256]{2,1,0:T(8,128)(2,1)S(1)}, bf16[6,128,256]{2,1,0:T(8,128)(2,1)}, u32[]{:S(2)}) copy-start(bf16[6,128,256]{2,1,0:T(8,128)(2,1)} %get-tuple-element.16.rowf_any.rowf_ref) | copy-start | bytes 1179652
  79.5 9.9 %collective-permute-start = (bf16[6,16,256]{2,1,0:T(8,128)(2,1)}, bf16[6,16,256]{2,1,0:T(8,128)(2,1)S(1)}, u32[]{:S(2)}, u32[]{:S(2)}) collective-permute-start(bf16[6,16,256]{2,1,0:T(8,128)(2,1)} %get-tuple-element.19), channel_id=1, source_target_pairs={{0,1},{1,2},{2,3},{3,4},{4,5},{5,6},{6,7},{8,9},{9,10},{10,11},{11... | collective-permute-start | bytes 147464 | tf_op jit(solution)/shard_map/ppermute | solution.py:524
  87.4 7.1 %collective-permute-start.1 = (bf16[6,16,256]{2,1,0:T(8,128)(2,1)}, bf16[6,16,256]{2,1,0:T(8,128)(2,1)S(1)}, u32[]{:S(2)}, u32[]{:S(2)}) collective-permute-start(bf16[6,16,256]{2,1,0:T(8,128)(2,1)} %get-tuple-element.20), channel_id=1, source_target_pairs={{1,0},{2,1},{3,2},{4,3},{5,4},{6,5},{7,6},{9,8},{10,9},{11,10},{12... | collective-permute-start | bytes 147464 | tf_op jit(solution)/shard_map/ppermute | solution.py:525

commit v3 on v2

--- a/solution.py
+++ b/solution.py
@@ -199,7 +199,8 @@
 
 
 def bands_kernel(
-    oy_ref, coef_ref, taps_ref, psf_ref, down_ref, colf_ref, rowf_ref, toep_ref, shift_ref,
+    oy_ref, coef_ref, taps_ref, psf_ref,
+    near_ref, far_ref, colf_ref, rowf_ref, down_ref, toep_ref, shift_ref,
 ):
     v = pl.program_id(0)
 
@@ -247,45 +248,49 @@
             ends = []
             for q in range(3):
                 low, high = sums[q * 2], sums[q * 2 + 1]
-                down_ref[0, pl.ds(q * SIDE + g * 16, 16), i * 128 : (i + 1) * 128] = (
+                down_ref[pl.ds(q * SIDE + g * 16, 16), i * 128 : (i + 1) * 128] = (
                     low + jnp.where(three, quarter(high, -1), 0.0)
                 ).astype(bf16)
                 ends.append(quarter(high, i))
             fifth.append(ends)
         for q in range(3):
             row_at = pl.ds(q * SIDE + g * 16, 16)
-            down_ref[0, row_at, 768:896] = choose(masks, *(fifth[i][q] for i in range(4))).astype(
+            down_ref[row_at, 768:896] = choose(masks, *(fifth[i][q] for i in range(4))).astype(
                 bf16
             )
             gap = jnp.zeros((16, 128), f32)
-            down_ref[0, row_at, 896:1024] = choose(
+            down_ref[row_at, 896:1024] = choose(
                 masks, fifth[4][q], fifth[5][q], gap, gap
             ).astype(bf16)
         return 0
 
     lax.fori_loop(0, SIDE // 16, step, 0)
 
+    @pl.when(v < 3)
+    def _():
+        near_ref[v] = down_ref[...]
+
+    @pl.when(v >= 3)
+    def _():
+        far_ref[0] = down_ref[...]
+
 
 def model_kernel(
-    ox_ref, rows_ref, across_any, down_any, colf_any, rowf_any, sci_any,
-    diff_any, score_any, part_ref, top_ref, bot_ref,
-    across_ref, down_ref, colf_ref, rowf_ref, sci_ref, diff_ref, score_ref,
-    win_ref, stack_ref, sem, out_sem,
+    ox_ref, rows_ref, down_ref, across_any, far_any, colf_any, sci_any,
+    diff_any, filt_any, top_ref, bot_ref,
+    across_ref, far_ref, colf_ref, sci_ref, diff_ref, filt_ref, win_ref, stack_ref, sem, out_sem,
 ):
-    band = pltpu.make_async_copy(across_any, across_ref, sem.at[VISITS, 0])
-    band.start()
-    fetch = [
-        [
-            pltpu.make_async_copy(src.at[v], dst.at[v], sem.at[v, k])
-            for k, (src, dst) in enumerate(
-                ((down_any, down_ref), (colf_any, colf_ref), (rowf_any, rowf_ref), (sci_any, sci_ref))
+    whole = [
+        pltpu.make_async_copy(src, dst, sem.at[k])
+        for k, (src, dst) in enumerate(
+            (
+                (across_any, across_ref), (colf_any, colf_ref), (sci_any, sci_ref),
+                (far_any, far_ref),
             )
-        ]
-        for v in range(VISITS)
+        )
     ]
-    for copies in fetch:
-        for copy in copies:
-            copy.start()
+    for copy in whole:
+        copy.start()
     half = GROUP // 2
     move = gather_rows()
     masks = quarter_masks(half)
@@ -357,43 +362,69 @@
                     stack_ref[v, i * 128 : (i + 1) * 128, cols] = piece[0:128]
                     stack_ref[v, low : low + half, cols] = piece[128:160]
 
-    def finish(v):
-        parts = jnp.dot(down_ref[v], stack_ref[v], preferred_element_type=f32)
+    def differ(v):
+        down = down_ref[v] if v < 3 else far_ref[v - 3]
+        parts = jnp.dot(down, stack_ref[v], preferred_element_type=f32)
         model = parts[0:128] + tx * (parts[128:256] + tx * parts[256:384])
-        diff = (sci_ref[v].astype(f32) - model).astype(bf16)
-        diff_ref[v] = diff
-        filt = jnp.dot(diff, colf_ref[v], preferred_element_type=f32).astype(bf16)
+        diff_ref[v] = (sci_ref[v].astype(f32) - model).astype(bf16)
+
+    def columns(v):
+        filt = jnp.dot(diff_ref[v], colf_ref[v], preferred_element_type=f32).astype(bf16)
+        filt_ref[v] = filt
         top_ref[v] = filt[0:HALO]
         bot_ref[v] = filt[SIDE - HALO :]
-        score = jnp.dot(rowf_ref[v, :, 0:128], filt, preferred_element_type=f32)
+
+    def send(group, k, src, dst):
+        copy = pltpu.make_async_copy(
+            src.at[group[0] : group[-1] + 1], dst.at[group[0] : group[-1] + 1], out_sem.at[k]
+        )
+        copy.start()
+        out.append(copy)
+
+    early, rest = (0, 1, 2), (3, 4, 5)
+    for v in early:
+        window(v)
+    whole[0].wait()
+    spread(early)
+    for v in rest:
+        window(v)
+    spread(rest)
+    for copy in whole[1:3]:
+        copy.wait()
+    for v in early:
+        differ(v)
+    for v in early:
+        columns(v)
+    whole[3].wait()
+    send(early, 0, diff_ref, diff_any)
+    send(early, 1, filt_ref, filt_any)
+    for v in rest:
+        differ(v)
+    send(rest, 2, diff_ref, diff_any)
+    for v in rest:
+        columns(v)
+    send(rest, 3, filt_ref, filt_any)
+    for copy in out:
+        copy.wait()
+
+
+def score_kernel(filt_any, rowf_any, score_any, part_ref, filt_ref, rowf_ref, score_ref, sem):
+    fetch = [
+        pltpu.make_async_copy(filt_any, filt_ref, sem.at[0]),
+        pltpu.make_async_copy(rowf_any, rowf_ref, sem.at[1]),
+    ]
+    for copy in fetch:
+        copy.start()
+    for copy in fetch:
+        copy.wait()
+    for v in range(VISITS):
+        score = jnp.dot(rowf_ref[v, :, 0:128], filt_ref[v], preferred_element_type=f32)
         score_ref[v] = score
         part_ref[v, 0:HALO] = score[0:HALO]
         part_ref[v, HALO:] = score[SIDE - HALO :]
-        out.append(pltpu.make_async_copy(diff_ref.at[v], diff_any.at[v], out_sem.at[v, 0]))
-        out.append(pltpu.make_async_copy(score_ref.at[v], score_any.at[v], out_sem.at[v, 1]))
-        out[-2].start()
-        out[-1].start()
-
-    early, rest = (0, 1, 2), (3, 4, 5)
-    for v in early:
-        window(v)
-    band.wait()
-    spread(early)
-    for v in rest:
-        window(v)
-    for v in early:
-        for copy in fetch[v]:
-            copy.wait()
-    spread(rest)
-    for v in early:
-        finish(v)
-    for v in rest:
-        for copy in fetch[v]:
-            copy.wait()
-    for v in rest:
-        finish(v)
-    for copy in out:
-        copy.wait()
+    out = pltpu.make_async_copy(score_ref, score_any, sem.at[2])
+    out.start()
+    out.wait()
 
 
 def edge_kernel(part_ref, above_ref, below_ref, rowf_ref, _, score_ref, buf_ref, sem):
@@ -431,7 +462,7 @@
 
     packed = pl.pallas_call(
         pack_kernel,
-        out_shape=sds((GROUP // 2, 2, PACKED, 128), bf16),
+        out_shape=pltpu.VMEM((GROUP // 2, 2, PACKED, 128), bf16),
         in_specs=[HB] * 5,
         out_specs=VM,
         scratch_shapes=[
@@ -456,7 +487,7 @@
     rowrow = jnp.concatenate([psf[:, 0], zero], axis=1)
     psf_rows = jnp.stack([jnp.roll(colrow, -RAD, axis=1), jnp.roll(rowrow, -RAD, axis=1)], axis=1)
 
-    down, colf, rowf = pl.pallas_call(
+    down, far, colf, rowf = pl.pallas_call(
         bands_kernel,
         grid=(VISITS,),
         in_specs=[
@@ -465,22 +496,25 @@
             pl.BlockSpec((1, 2, FAR), lambda v: (v, 0, 0)),
         ],
         out_specs=[
-            pl.BlockSpec((1, 384, LONG), lambda v: (v, 0, 0)),
+            VM,
+            pl.BlockSpec((1, 384, LONG), lambda v: (jnp.maximum(v - 3, 0), 0, 0)),
             pl.BlockSpec((1, COLS, COLS), lambda v: (v, 0, 0)),
             pl.BlockSpec((1, SIDE, FAR), lambda v: (v, 0, 0)),
         ],
         out_shape=[
-            sds((VISITS, 384, LONG), bf16),
+            pltpu.VMEM((3, 384, LONG), bf16),
+            sds((3, 384, LONG), bf16),
             sds((VISITS, COLS, COLS), bf16),
             sds((VISITS, SIDE, FAR), bf16),
         ],
         scratch_shapes=[
+            pltpu.VMEM((384, LONG), bf16),
             pltpu.VMEM((ORDERS, SIDE, FAR), f32),
             pltpu.VMEM((ORDERS, SIDE, FAR), f32),
         ],
         name="bands",
     )(oy, coefficients.reshape(VISITS, 126), jnp.asarray(ahead), psf_rows)
-    stripes, down = lax.optimization_barrier((stripes, down))
+    stripes, colf = lax.optimization_barrier((stripes, colf))
 
     picked = pl.pallas_call(
         select_kernel,
@@ -493,36 +527,52 @@
     )(me, near(stripes))
     rows = lax.all_to_all(picked, "sky", 0, 0, tiled=True)
 
-    difference, score, part, top, bot = pl.pallas_call(
+    difference, filtered, top, bot = pl.pallas_call(
         model_kernel,
-        in_specs=[SM, VM] + [HB] * 5,
-        out_specs=[HB, HB, VM, VM, VM],
+        in_specs=[SM, VM, VM] + [HB] * 4,
+        out_specs=[HB, HB, VM, VM],
         out_shape=[
             sds((VISITS, SIDE, COLS), bf16),
-            sds((VISITS, SIDE, COLS), f32),
-            pltpu.VMEM((VISITS, 2 * HALO, COLS), f32),
+            sds((VISITS, SIDE, COLS), bf16),
             sds((VISITS, HALO, COLS), bf16),
             sds((VISITS, HALO, COLS), bf16),
         ],
         scratch_shapes=[
             pltpu.VMEM((FAR, 768), bf16),
-            pltpu.VMEM((VISITS, 384, LONG), bf16),
+            pltpu.VMEM((3, 384, LONG), bf16),
             pltpu.VMEM((VISITS, COLS, COLS), bf16),
-            pltpu.VMEM((VISITS, SIDE, FAR), bf16),
             pltpu.VMEM((VISITS, SIDE, COLS), bf16),
             pltpu.VMEM((VISITS, SIDE, COLS), bf16),
-            pltpu.VMEM((VISITS, SIDE, COLS), f32),
+            pltpu.VMEM((VISITS, SIDE, COLS), bf16),
             pltpu.VMEM((VISITS * 320, 256), bf16),
             pltpu.VMEM((VISITS, LONG, COLS), bf16),
-            pltpu.SemaphoreType.DMA((VISITS + 1, 4)),
-            pltpu.SemaphoreType.DMA((VISITS, 2)),
+            pltpu.SemaphoreType.DMA((4,)),
+            pltpu.SemaphoreType.DMA((4,)),
         ],
         name="model",
-    )(ox, near(rows), jnp.asarray(across_band(taps)).astype(bf16), down, colf, rowf, science)
+    )(ox, near(rows), near(down), jnp.asarray(across_band(taps)).astype(bf16), far, colf, science)
 
     count = lax.axis_size("ccd")
     above = lax.ppermute(bot, "ccd", [(i, i + 1) for i in range(count - 1)])
     below = lax.ppermute(top, "ccd", [(i + 1, i) for i in range(count - 1)])
+
+    score, part = pl.pallas_call(
+        score_kernel,
+        in_specs=[HB, HB],
+        out_specs=[HB, VM],
+        out_shape=[
+            sds((VISITS, SIDE, COLS), f32),
+            pltpu.VMEM((VISITS, 2 * HALO, COLS), f32),
+        ],
+        scratch_shapes=[
+            pltpu.VMEM((VISITS, SIDE, COLS), bf16),
+            pltpu.VMEM((VISITS, SIDE, FAR), bf16),
+            pltpu.VMEM((VISITS, SIDE, COLS), f32),
+            pltpu.SemaphoreType.DMA((3,)),
+        ],
+        name="score",
+    )(filtered, rowf)
+
     score = pl.pallas_call(
         edge_kernel,
         out_shape=sds((VISITS, SIDE, COLS), f32),

time: 95.8 us -> 92.8 us (0.969)
  the two profiles are of different devices: /device:TPU:24 before, /device:TPU:8 now
where the time goes in v3:
time: 92.8 us; the launch traced here: 92.5 us
  Pallas kernels  28.3 us (30%)
  blocking collectives  27.4 us (30%)
  starting transfers between devices  25.8 us (28%)
  waiting for transfers between devices  8.26 us (9%)
  local copies, waits for them, and re-layouts  1.21 us (1%)
    all_to_all x1, blocking collectives, body(): rows = lax.all_to_all(picked, 'sky', 0, 0, tiled=True)  27.4 us
    all_to_all x1, starting transfers between devices, body(): lax.all_to_all(packed.reshape(GROUP, PACKED, 128), 'sky', 0, 0, tiled=True)  15.7 us
    pallas_call x1, Pallas kernels, body(): pl.pallas_call(bands_kernel, grid=(VISITS,), in_specs=[SM, SM, pl.BlockSp...  14 us
    ppermute x1, starting transfers between devices, body(): above = lax.ppermute(bot, 'ccd', [(i, i + 1) for i in range(count - 1)])  8.14 us
    pallas_call x1, Pallas kernels, body(): pl.pallas_call(model_kernel, in_specs=[SM, VM, VM] + [HB] * 4, out_specs=...  6.54 us
    all_to_all x1, waiting for transfers between devices, body(): lax.all_to_all(packed.reshape(GROUP, PACKED, 128), 'sky', 0, 0, tiled=True)  5.39 us
    ppermute x1, waiting for transfers between devices, body(): below = lax.ppermute(top, 'ccd', [(i + 1, i) for i in range(count - 1)])  2.87 us
    pallas_call x1, Pallas kernels, body(): pl.pallas_call(pack_kernel, out_shape=pltpu.VMEM((GROUP // 2, 2, PACKED,...  2.69 us
  transfers between devices with their start and end apart: 3, of which 2 were waited for; matrix products, arithmetic and copies ran while one was open for 2% of the time, Pallas kernels for 18%

profile of v3, /device:TPU:8, one launch (start us, length us, event | category | flops | bytes accessed | tf_op | source)
XLA Modules:
  0.0 92.5 jit_solution(12312211310175319613)
XLA Ops:
  0.6 0.0 copy-start.2
  0.6 0.0 copy-start.1
  0.7 2.7 %pack.1 = bf16[32,2,40,128]{3,2,1,0:T(8,128)(2,1)} custom-call(bf16[16,128,128]{2,1,0:T(8,128)(2,1)} %cells_any.1, s32[1,36]{1,0:T(1,128)} %bitcast.21, s32[1,36]{1,0:T(1,128)} %index_any.1, s32[1,6]{1,0:T(1,128)} %bitcast.19, s32[1,6]{1,0:T(1,128)} %bitcast.17), custom_call_target="tpu_custom_call" | custom-call | tf_op jit(solution)/shard_map/pack/pallas_call | solution.py:463
  3.3 15.7 %all-to-all-start = ((bf16[64,40,128]{2,1,0:T(8,128)(2,1)}), bf16[64,40,128]{2,1,0:T(8,128)(2,1)S(1)}, u32[]{:S(2)}, u32[]{:S(2)}) async-start(bf16[64,40,128]{2,1,0:T(8,128)(2,1)} %bitcast.5), calls=%async_computation | async-start | bytes 1310720 | tf_op jit(solution)/shard_map/all_to_all | solution.py:479
  19.1 0.0 copy-done.2
  19.1 0.1 slice.27
  19.2 0.1 rev.4
  19.2 0.1 slice.28
  19.3 0.1 pad_slice_fusion.1
  19.4 0.1 maximum_bitcast_fusion
  19.5 0.1 pad_slice_fusion
  19.5 0.1 pad_maximum_fusion.1
  19.6 0.0 copy-done.1
  19.6 0.1 copy.16
  19.8 0.7 reshape.19.coef_ref
  20.4 0.6 pad_maximum_fusion.psf_ref
  21.1 14.0 %bands.1 = (bf16[3,384,1024]{2,1,0:T(8,128)(2,1)S(1)}, bf16[3,384,1024]{2,1,0:T(8,128)(2,1)}, bf16[6,256,256]{2,1,0:T(8,128)(2,1)}, bf16[6,128,256]{2,1,0:T(8,128)(2,1)}) custom-call(s32[6]{0:T(128)} %bitcast.20, f32[6,126]{1,0:T(8,128)} %reshape.19.coef_ref, f32[8,256]{1,0:T(8,128)} %constant.12.clone.taps_ref, f32[6,2,256]{2,1,0:T(2,128)} %pad_maximum_fusion.psf_ref), custom_call_target="tpu_custom_call" | custom-call | tf_op jit(solution)/shard_map/bands/pallas_call | solution.py:490
  35.1 5.4 %all-to-all-done.stripes_ref = bf16[64,40,128]{2,1,0:T(8,128)(2,1)S(1)} async-done(((bf16[64,40,128]{2,1,0:T(8,128)(2,1)}), bf16[64,40,128]{2,1,0:T(8,128)(2,1)S(1)}, u32[]{:S(2)}, u32[]{:S(2)}) %all-to-all-start) | async-done | bytes 655392 | tf_op jit(solution)/shard_map/all_to_all | solution.py:479
  40.5 1.9 %select.3 = bf16[64,40,128]{2,1,0:T(8,128)(2,1)S(1)} custom-call(s32[1]{0:T(128)} %bitcast.1.me_ref, bf16[64,40,128]{2,1,0:T(8,128)(2,1)S(1)} %all-to-all-done.stripes_ref), custom_call_target="tpu_custom_call" | custom-call | tf_op jit(solution)/shard_map/select/pallas_call | solution.py:519
  42.4 27.4 %all_to_all.10.rows_ref = bf16[64,40,128]{2,1,0:T(8,128)(2,1)S(1)} all-to-all(bf16[64,40,128]{2,1,0:T(8,128)(2,1)S(1)} %select.3), channel_id=1, replica_groups=mesh['sky'=64,'ccd'=8] {'sky'}, dimensions={0} | all-to-all | bytes 1310720 | tf_op jit(solution)/shard_map/all_to_all | solution.py:528
  69.8 0.0 copy-start
  69.8 6.5 %model.1 = (bf16[6,128,256]{2,1,0:T(8,128)(2,1)}, bf16[6,128,256]{2,1,0:T(8,128)(2,1)}, bf16[6,16,256]{2,1,0:T(8,128)(2,1)}, bf16[6,16,256]{2,1,0:T(8,128)(2,1)}) custom-call(s32[6]{0:T(128)} %bitcast.18, bf16[64,40,128]{2,1,0:T(8,128)(2,1)S(1)} %all_to_all.10.rows_ref, bf16[3,384,1024]{2,1,0:T(8,128)(2,1)S(1)} %get-tuple-element.16.down_ref, ...), custom_call_target="tpu_custom_call" | custom-call | tf_op jit(solution)/shard_map/model/pallas_call | solution.py:530
  76.4 8.1 %collective-permute-start = (bf16[6,16,256]{2,1,0:T(8,128)(2,1)}, bf16[6,16,256]{2,1,0:T(8,128)(2,1)S(1)}, u32[]{:S(2)}, u32[]{:S(2)}) collective-permute-start(bf16[6,16,256]{2,1,0:T(8,128)(2,1)} %get-tuple-element.23), channel_id=1, source_target_pairs={{0,1},{1,2},{2,3},{3,4},{4,5},{5,6},{6,7},{8,9},{9,10},{10,11},{11... | collective-permute-start | bytes 147464 | tf_op jit(solution)/shard_map/ppermute | solution.py:556
  84.5 1.9 %collective-permute-start.1 = (bf16[6,16,256]{2,1,0:T(8,128)(2,1)}, bf16[6,16,256]{2,1,0:T(8,128)(2,1)S(1)}, u32[]{:S(2)}, u32[]{:S(2)}) collective-permute-start(bf16[6,16,256]{2,1,0:T(8,128)(2,1)} %get-tuple-element.24), channel_id=1, source_target_pairs={{1,0},{2,1},{3,2},{4,3},{5,4},{6,5},{7,6},{9,8},{10,9},{11,10},{12... | collective-permute-start | bytes 147464 | tf_op jit(solution)/shard_map/ppermute | solution.py:557
  86.4 2.3 %score.1 = (f32[6,128,256]{2,1,0:T(8,128)}, f32[6,32,256]{2,1,0:T(8,128)S(1)}) custom-call(bf16[6,128,256]{2,1,0:T(8,128)(2,1)} %get-tuple-element.20.filt_any, bf16[6,128,256]{2,1,0:T(8,128)(2,1)} %get-tuple-element.21.rowf_any.rowf_ref), custom_call_target="tpu_custom_call" | custom-call | tf_op jit(solution)/shard_map/score/pallas_call | solution.py:559
  88.7 0.0 collective-permute-done.above_ref
  88.7 2.9 %collective-permute-done.1.below_ref = bf16[6,16,256]{2,1,0:T(8,128)(2,1)S(1)} collective-permute-done((bf16[6,16,256]{2,1,0:T(8,128)(2,1)}, bf16[6,16,256]{2,1,0:T(8,128)(2,1)S(1)}, u32[]{:S(2)}, u32[]{:S(2)}) %collective-permute-start.1) | collective-permute-done | bytes 49184 | tf_op jit(solution)/shard_map/ppermute | solution.py:557
  91.6 0.0 copy-done
  91.6 0.9 edges.1
  (4 shorter events, 0.0 us)
Async XLA Ops:
  0.6 18.4 %copy-start.2 = (bf16[6,2,31]{2,1,0:T(2,128)(2,1)S(1)}, bf16[6,2,31]{2,1,0:T(2,128)(2,1)}, u32[]{:S(2)}) copy-start(bf16[6,2,31]{2,1,0:T(2,128)(2,1)} %param.17) | copy-start | bytes 2236
  0.6 19.0 %copy-start.1 = (f32[6,1,21,6]{2,1,3,0:T(1,128)S(1)}, f32[6,1,21,6]{2,1,3,0:T(1,128)}, u32[]{:S(2)}) copy-start(f32[6,1,21,6]{2,1,3,0:T(1,128)} %param.16) | copy-start | bytes 9076
  3.3 37.1 %all-to-all-start = ((bf16[64,40,128]{2,1,0:T(8,128)(2,1)}), bf16[64,40,128]{2,1,0:T(8,128)(2,1)S(1)}, u32[]{:S(2)}, u32[]{:S(2)}) async-start(bf16[64,40,128]{2,1,0:T(8,128)(2,1)} %bitcast.5), calls=%async_computation | async-start | bytes 1310720 | tf_op jit(solution)/shard_map/all_to_all | solution.py:479
  69.8 21.8 %copy-start = (bf16[6,128,256]{2,1,0:T(8,128)(2,1)S(1)}, bf16[6,128,256]{2,1,0:T(8,128)(2,1)}, u32[]{:S(2)}) copy-start(bf16[6,128,256]{2,1,0:T(8,128)(2,1)} %get-tuple-element.21.rowf_any.rowf_ref) | copy-start | bytes 1179652
  76.4 12.4 %collective-permute-start = (bf16[6,16,256]{2,1,0:T(8,128)(2,1)}, bf16[6,16,256]{2,1,0:T(8,128)(2,1)S(1)}, u32[]{:S(2)}, u32[]{:S(2)}) collective-permute-start(bf16[6,16,256]{2,1,0:T(8,128)(2,1)} %get-tuple-element.23), channel_id=1, source_target_pairs={{0,1},{1,2},{2,3},{3,4},{4,5},{5,6},{6,7},{8,9},{9,10},{10,11},{11... | collective-permute-start | bytes 147464 | tf_op jit(solution)/shard_map/ppermute | solution.py:556
  84.5 7.1 %collective-permute-start.1 = (bf16[6,16,256]{2,1,0:T(8,128)(2,1)}, bf16[6,16,256]{2,1,0:T(8,128)(2,1)S(1)}, u32[]{:S(2)}, u32[]{:S(2)}) collective-permute-start(bf16[6,16,256]{2,1,0:T(8,128)(2,1)} %get-tuple-element.24), channel_id=1, source_target_pairs={{1,0},{2,1},{3,2},{4,3},{5,4},{6,5},{7,6},{9,8},{10,9},{11,10},{12... | collective-permute-start | bytes 147464 | tf_op jit(solution)/shard_map/ppermute | solution.py:557

commit v4 on v3

--- a/solution.py
+++ b/solution.py
@@ -84,24 +84,27 @@
 
 
 def pack_kernel(
-    cells_any, owner_any, index_any, oy_any, ox_any, out_ref,
-    cells_ref, owner_ref, index_ref, oy_ref, ox_ref, info_ref, sem,
+    cells_any, owner_any, index_any, oy_any, ox_any, out_any,
+    cells_ref, owner_ref, index_ref, oy_ref, ox_ref, info_ref, out_ref, sem, out_sem,
 ):
-    copies = [
-        pltpu.make_async_copy(src, dst, sem.at[k])
+    cells = [
+        pltpu.make_async_copy(
+            cells_any.at[h * 8 : (h + 1) * 8], cells_ref.at[h * 8 : (h + 1) * 8], sem.at[h]
+        )
+        for h in range(2)
+    ]
+    small = [
+        pltpu.make_async_copy(src, dst, sem.at[2 + k])
         for k, (src, dst) in enumerate(
-            (
-                (cells_any, cells_ref), (owner_any, owner_ref), (index_any, index_ref),
-                (oy_any, oy_ref), (ox_any, ox_ref),
-            )
+            ((owner_any, owner_ref), (index_any, index_ref), (oy_any, oy_ref), (ox_any, ox_ref))
         )
     ]
-    for copy in copies:
+    for copy in cells + small:
         copy.start()
     move = scatter_rows()
     masks = quarter_masks(256)
     info_ref[...] = jnp.zeros((8, 128), f32)
-    for copy in copies[1:]:
+    for copy in small:
         copy.wait()
     info_ref[0:1, 0:36] = owner_ref[...].astype(f32)
     info_ref[1:2, 0:36] = index_ref[...].astype(f32)
@@ -110,22 +113,34 @@
     info = info_ref[...].astype(bf16)
     for d in range(GROUP):
         out_ref[d // 2, d % 2, STRIPE:PACKED, :] = info
-    copies[0].wait()
-    moved = []
-    for q in range(4):
-        halves = [
-            cells_ref[h * 8 : (h + 1) * 8, q * 32 : (q + 1) * 32, :].reshape(256, 128)
-            for h in range(2)
+    out = []
+
+    def send(at):
+        copy = pltpu.make_async_copy(
+            out_ref.at[:, :, at : at + 8], out_any.at[:, :, at : at + 8], out_sem.at[at // 8]
+        )
+        copy.start()
+        out.append(copy)
+
+    send(STRIPE)
+    for h in range(2):
+        cells[h].wait()
+        moved = [
+            jnp.dot(
+                move,
+                cells_ref[h * 8 : (h + 1) * 8, q * 32 : (q + 1) * 32, :].reshape(256, 128),
+                preferred_element_type=f32,
+            )
+            for q in range(4)
         ]
-        moved.append(
-            jnp.dot(move, jnp.concatenate(halves, axis=1), preferred_element_type=f32)
-        )
-    for h in range(2):
-        groups = transpose_quarters([m[:, h * 128 : (h + 1) * 128] for m in moved], masks)
-        for c in range(2):
-            for u in range(2):
-                at = u * CELLS + h * 8
+        groups = transpose_quarters(moved, masks)
+        for u in range(2):
+            at = u * CELLS + h * 8
+            for c in range(2):
                 out_ref[:, c, at : at + 8, :] = groups[c + 2 * u].reshape(32, 8, 128).astype(bf16)
+            send(at)
+    for copy in out:
+        copy.wait()
 
 
 def select_kernel(me_ref, stripes_ref, out_ref, asks_ref):
@@ -268,7 +283,7 @@
 
     @pl.when(v < 3)
     def _():
-        near_ref[v] = down_ref[...]
+        near_ref[0] = down_ref[...]
 
     @pl.when(v >= 3)
     def _():
@@ -277,8 +292,8 @@
 
 def model_kernel(
     ox_ref, rows_ref, down_ref, across_any, far_any, colf_any, sci_any,
-    diff_any, filt_any, top_ref, bot_ref,
-    across_ref, far_ref, colf_ref, sci_ref, diff_ref, filt_ref, win_ref, stack_ref, sem, out_sem,
+    diff_ref, filt_ref, top_ref, bot_ref,
+    across_ref, far_ref, colf_ref, sci_ref, win_ref, stack_ref, sem,
 ):
     whole = [
         pltpu.make_async_copy(src, dst, sem.at[k])
@@ -289,7 +304,7 @@
             )
         )
     ]
-    for copy in whole:
+    for copy in whole[:3]:
         copy.start()
     half = GROUP // 2
     move = gather_rows()
@@ -344,7 +359,6 @@
 
     col = lax.broadcasted_iota(jnp.int32, (SIDE, COLS), 1).astype(f32)
     tx = (2.0 * col + 1.0) / COLS - 1.0
-    out = []
 
     def spread(group):
         at = group[0] * 320
@@ -374,17 +388,11 @@
         top_ref[v] = filt[0:HALO]
         bot_ref[v] = filt[SIDE - HALO :]
 
-    def send(group, k, src, dst):
-        copy = pltpu.make_async_copy(
-            src.at[group[0] : group[-1] + 1], dst.at[group[0] : group[-1] + 1], out_sem.at[k]
-        )
-        copy.start()
-        out.append(copy)
-
     early, rest = (0, 1, 2), (3, 4, 5)
     for v in early:
         window(v)
     whole[0].wait()
+    whole[3].start()
     spread(early)
     for v in rest:
         window(v)
@@ -396,35 +404,27 @@
     for v in early:
         columns(v)
     whole[3].wait()
-    send(early, 0, diff_ref, diff_any)
-    send(early, 1, filt_ref, filt_any)
     for v in rest:
         differ(v)
-    send(rest, 2, diff_ref, diff_any)
     for v in rest:
         columns(v)
-    send(rest, 3, filt_ref, filt_any)
-    for copy in out:
-        copy.wait()
-
-
-def score_kernel(filt_any, rowf_any, score_any, part_ref, filt_ref, rowf_ref, score_ref, sem):
-    fetch = [
-        pltpu.make_async_copy(filt_any, filt_ref, sem.at[0]),
-        pltpu.make_async_copy(rowf_any, rowf_ref, sem.at[1]),
-    ]
-    for copy in fetch:
-        copy.start()
-    for copy in fetch:
-        copy.wait()
+
+
+def score_kernel(filt_ref, diff_ref, rowf_any, diff_any, score_any, part_ref, rowf_ref, score_ref, sem):
+    rows = pltpu.make_async_copy(rowf_any, rowf_ref, sem.at[0])
+    keep = pltpu.make_async_copy(diff_ref, diff_any, sem.at[1])
+    rows.start()
+    keep.start()
+    rows.wait()
     for v in range(VISITS):
         score = jnp.dot(rowf_ref[v, :, 0:128], filt_ref[v], preferred_element_type=f32)
         score_ref[v] = score
         part_ref[v, 0:HALO] = score[0:HALO]
         part_ref[v, HALO:] = score[SIDE - HALO :]
-    out = pltpu.make_async_copy(score_ref, score_any, sem.at[2])
-    out.start()
-    out.wait()
+    done = pltpu.make_async_copy(score_ref, score_any, sem.at[2])
+    done.start()
+    keep.wait()
+    done.wait()
 
 
 def edge_kernel(part_ref, above_ref, below_ref, rowf_ref, _, score_ref, buf_ref, sem):
@@ -462,9 +462,9 @@
 
     packed = pl.pallas_call(
         pack_kernel,
-        out_shape=pltpu.VMEM((GROUP // 2, 2, PACKED, 128), bf16),
+        out_shape=sds((GROUP // 2, 2, PACKED, 128), bf16),
         in_specs=[HB] * 5,
-        out_specs=VM,
+        out_specs=HB,
         scratch_shapes=[
             pltpu.VMEM((CELLS, SIDE, 128), bf16),
             pltpu.VMEM((1, 36), jnp.int32),
@@ -472,6 +472,8 @@
             pltpu.VMEM((1, VISITS), jnp.int32),
             pltpu.VMEM((1, VISITS), jnp.int32),
             pltpu.VMEM((8, 128), f32),
+            pltpu.VMEM((GROUP // 2, 2, PACKED, 128), bf16),
+            pltpu.SemaphoreType.DMA((6,)),
             pltpu.SemaphoreType.DMA((5,)),
         ],
         name="pack",
@@ -496,13 +498,13 @@
             pl.BlockSpec((1, 2, FAR), lambda v: (v, 0, 0)),
         ],
         out_specs=[
-            VM,
+            pl.BlockSpec((1, 384, LONG), lambda v: (jnp.minimum(v, 2), 0, 0)),
             pl.BlockSpec((1, 384, LONG), lambda v: (jnp.maximum(v - 3, 0), 0, 0)),
             pl.BlockSpec((1, COLS, COLS), lambda v: (v, 0, 0)),
             pl.BlockSpec((1, SIDE, FAR), lambda v: (v, 0, 0)),
         ],
         out_shape=[
-            pltpu.VMEM((3, 384, LONG), bf16),
+            sds((3, 384, LONG), bf16),
             sds((3, 384, LONG), bf16),
             sds((VISITS, COLS, COLS), bf16),
             sds((VISITS, SIDE, FAR), bf16),
@@ -527,13 +529,13 @@
     )(me, near(stripes))
     rows = lax.all_to_all(picked, "sky", 0, 0, tiled=True)
 
-    difference, filtered, top, bot = pl.pallas_call(
+    near_diff, filtered, top, bot = pl.pallas_call(
         model_kernel,
         in_specs=[SM, VM, VM] + [HB] * 4,
-        out_specs=[HB, HB, VM, VM],
+        out_specs=[VM] * 4,
         out_shape=[
-            sds((VISITS, SIDE, COLS), bf16),
-            sds((VISITS, SIDE, COLS), bf16),
+            pltpu.VMEM((VISITS, SIDE, COLS), bf16),
+            pltpu.VMEM((VISITS, SIDE, COLS), bf16),
             sds((VISITS, HALO, COLS), bf16),
             sds((VISITS, HALO, COLS), bf16),
         ],
@@ -542,13 +544,11 @@
             pltpu.VMEM((3, 384, LONG), bf16),
             pltpu.VMEM((VISITS, COLS, COLS), bf16),
             pltpu.VMEM((VISITS, SIDE, COLS), bf16),
-            pltpu.VMEM((VISITS, SIDE, COLS), bf16),
-            pltpu.VMEM((VISITS, SIDE, COLS), bf16),
             pltpu.VMEM((VISITS * 320, 256), bf16),
             pltpu.VMEM((VISITS, LONG, COLS), bf16),
             pltpu.SemaphoreType.DMA((4,)),
-            pltpu.SemaphoreType.DMA((4,)),
-        ],
+        ],
+        compiler_params=pltpu.CompilerParams(vmem_limit_bytes=61600 * 1024),
         name="model",
     )(ox, near(rows), near(down), jnp.asarray(across_band(taps)).astype(bf16), far, colf, science)
 
@@ -556,22 +556,23 @@
     above = lax.ppermute(bot, "ccd", [(i, i + 1) for i in range(count - 1)])
     below = lax.ppermute(top, "ccd", [(i + 1, i) for i in range(count - 1)])
 
-    score, part = pl.pallas_call(
+    difference, score, part = pl.pallas_call(
         score_kernel,
-        in_specs=[HB, HB],
-        out_specs=[HB, VM],
+        in_specs=[VM, VM, HB],
+        out_specs=[HB, HB, VM],
         out_shape=[
+            sds((VISITS, SIDE, COLS), bf16),
             sds((VISITS, SIDE, COLS), f32),
             pltpu.VMEM((VISITS, 2 * HALO, COLS), f32),
         ],
         scratch_shapes=[
-            pltpu.VMEM((VISITS, SIDE, COLS), bf16),
             pltpu.VMEM((VISITS, SIDE, FAR), bf16),
             pltpu.VMEM((VISITS, SIDE, COLS), f32),
             pltpu.SemaphoreType.DMA((3,)),
         ],
+        compiler_params=LIMIT,
         name="score",
-    )(filtered, rowf)
+    )(near(filtered), near(near_diff), rowf)
 
     score = pl.pallas_call(
         edge_kernel,

time: 92.8 us -> 94.1 us (1.014)
  local copies, waits for them, and re-layouts: 1.21 us -> 3.86 us
  Pallas kernels: 28.3 us -> 27 us
    unnamed x7 -> x9, local copies, waits for them, and re-layouts: 0.14 us -> 2.8 us
  transfers between devices with their start and end apart: 3 -> 3, of which waited for: 2 -> 2; matrix products, arithmetic and copies ran while one was open for 2% -> 2% of each run, Pallas kernels for 18% -> 17%
where the time goes in v4:
time: 94.1 us; the launch traced here: 93.7 us
  blocking collectives  27.8 us (30%)
  Pallas kernels  27 us (29%)
  starting transfers between devices  25.6 us (27%)
  waiting for transfers between devices  7.83 us (8%)
  local copies, waits for them, and re-layouts  3.86 us (4%)
    all_to_all x1, blocking collectives, body(): rows = lax.all_to_all(picked, 'sky', 0, 0, tiled=True)  27.8 us
    all_to_all x1, starting transfers between devices, body(): lax.all_to_all(packed.reshape(GROUP, PACKED, 128), 'sky', 0, 0, tiled=True)  15.7 us
    pallas_call x1, Pallas kernels, body(): pl.pallas_call(bands_kernel, grid=(VISITS,), in_specs=[SM, SM, pl.BlockSp...  14.4 us
    ppermute x1, starting transfers between devices, body(): above = lax.ppermute(bot, 'ccd', [(i, i + 1) for i in range(count - 1)])  8 us
    pallas_call x1, Pallas kernels, body(): pl.pallas_call(model_kernel, in_specs=[SM, VM, VM] + [HB] * 4, out_specs=...  5.67 us
    all_to_all x1, waiting for transfers between devices, body(): lax.all_to_all(packed.reshape(GROUP, PACKED, 128), 'sky', 0, 0, tiled=True)  5.02 us
    pallas_call x1, Pallas kernels, body(): pl.pallas_call(pack_kernel, out_shape=sds((GROUP // 2, 2, PACKED, 128), b...  2.84 us
    ppermute x1, waiting for transfers between devices, body(): below = lax.ppermute(top, 'ccd', [(i + 1, i) for i in range(count - 1)])  2.81 us
  transfers between devices with their start and end apart: 3, of which 2 were waited for; matrix products, arithmetic and copies ran while one was open for 2% of the time, Pallas kernels for 17%

profile of v4, /device:TPU:8, one launch (start us, length us, event | category | flops | bytes accessed | tf_op | source)
XLA Modules:
  0.0 93.7 jit_solution(10969146711458394787)
XLA Ops:
  0.6 0.0 copy-start.3
  0.6 0.0 copy-start.2
  0.7 2.8 %pack.1 = bf16[32,2,40,128]{3,2,1,0:T(8,128)(2,1)} custom-call(bf16[16,128,128]{2,1,0:T(8,128)(2,1)} %cells_any.1, s32[1,36]{1,0:T(1,128)} %bitcast.22, s32[1,36]{1,0:T(1,128)} %index_any.1, s32[1,6]{1,0:T(1,128)} %bitcast.20, s32[1,6]{1,0:T(1,128)} %bitcast.18), custom_call_target="tpu_custom_call" | custom-call | tf_op jit(solution)/shard_map/pack/pallas_call | solution.py:463
  3.5 15.7 %all-to-all-start = ((bf16[64,40,128]{2,1,0:T(8,128)(2,1)}), bf16[64,40,128]{2,1,0:T(8,128)(2,1)S(1)}, u32[]{:S(2)}, u32[]{:S(2)}) async-start(bf16[64,40,128]{2,1,0:T(8,128)(2,1)} %bitcast.16), calls=%async_computation | async-start | bytes 1310720 | tf_op jit(solution)/shard_map/all_to_all | solution.py:481
  19.2 0.0 copy-done.3
  19.2 0.1 slice.27
  19.3 0.1 rev.4
  19.4 0.1 slice.28
  19.5 0.1 pad_slice_fusion.1
  19.5 0.1 maximum_bitcast_fusion
  19.6 0.1 pad_slice_fusion
  19.7 0.1 pad_maximum_fusion.1
  19.8 0.0 copy-done.2
  19.8 0.1 copy.16
  19.9 0.7 reshape.19.coef_ref
  20.6 0.6 pad_maximum_fusion.psf_ref
  21.2 14.4 %bands.1 = (bf16[3,384,1024]{2,1,0:T(8,128)(2,1)}, bf16[3,384,1024]{2,1,0:T(8,128)(2,1)}, bf16[6,256,256]{2,1,0:T(8,128)(2,1)}, bf16[6,128,256]{2,1,0:T(8,128)(2,1)}) custom-call(s32[6]{0:T(128)} %bitcast.21, f32[6,126]{1,0:T(8,128)} %reshape.19.coef_ref, f32[8,256]{1,0:T(8,128)} %constant.12.clone.taps_ref, f32[6,2,256]{2,1,0:T(2,128)} %pad_maximum_fusion.psf_ref), custom_call_target="tpu_custom_call" | custom-call | tf_op jit(solution)/shard_map/bands/pallas_call | solution.py:492
  35.6 5.0 %all-to-all-done.stripes_ref = bf16[64,40,128]{2,1,0:T(8,128)(2,1)S(1)} async-done(((bf16[64,40,128]{2,1,0:T(8,128)(2,1)}), bf16[64,40,128]{2,1,0:T(8,128)(2,1)S(1)}, u32[]{:S(2)}, u32[]{:S(2)}) %all-to-all-start) | async-done | bytes 655392 | tf_op jit(solution)/shard_map/all_to_all | solution.py:481
  40.6 1.9 %select.3 = bf16[64,40,128]{2,1,0:T(8,128)(2,1)S(1)} custom-call(s32[1]{0:T(128)} %bitcast.1.me_ref, bf16[64,40,128]{2,1,0:T(8,128)(2,1)S(1)} %all-to-all-done.stripes_ref), custom_call_target="tpu_custom_call" | custom-call | tf_op jit(solution)/shard_map/select/pallas_call | solution.py:521
  42.5 27.8 %all_to_all.10.rows_ref = bf16[64,40,128]{2,1,0:T(8,128)(2,1)S(1)} all-to-all(bf16[64,40,128]{2,1,0:T(8,128)(2,1)S(1)} %select.3), channel_id=1, replica_groups=mesh['sky'=64,'ccd'=8] {'sky'}, dimensions={0} | all-to-all | bytes 1310720 | tf_op jit(solution)/shard_map/all_to_all | solution.py:530
  70.4 0.0 copy-start
  70.4 1.7 %copy-done = bf16[3,384,1024]{2,1,0:T(8,128)(2,1)S(1)} copy-done((bf16[3,384,1024]{2,1,0:T(8,128)(2,1)S(1)}, bf16[3,384,1024]{2,1,0:T(8,128)(2,1)}, u32[]{:S(2)}) %copy-start) | copy-done | bytes 2359320
  72.0 5.7 %model.1 = (bf16[6,128,256]{2,1,0:T(8,128)(2,1)S(1)}, bf16[6,128,256]{2,1,0:T(8,128)(2,1)S(1)}, bf16[6,16,256]{2,1,0:T(8,128)(2,1)}, bf16[6,16,256]{2,1,0:T(8,128)(2,1)}) custom-call(s32[6]{0:T(128)} %bitcast.19, bf16[64,40,128]{2,1,0:T(8,128)(2,1)S(1)} %all_to_all.10.rows_ref, bf16[3,384,1024]{2,1,0:T(8,128)(2,1)S(1)} %copy-done, ...), custom_call_target="tpu_custom_call" | custom-call | tf_op jit(solution)/shard_map/model/pallas_call | solution.py:532
  77.7 8.0 %collective-permute-start = (bf16[6,16,256]{2,1,0:T(8,128)(2,1)}, bf16[6,16,256]{2,1,0:T(8,128)(2,1)S(1)}, u32[]{:S(2)}, u32[]{:S(2)}) collective-permute-start(bf16[6,16,256]{2,1,0:T(8,128)(2,1)} %get-tuple-element.25), channel_id=1, source_target_pairs={{0,1},{1,2},{2,3},{3,4},{4,5},{5,6},{6,7},{8,9},{9,10},{10,11},{11... | collective-permute-start | bytes 147464 | tf_op jit(solution)/shard_map/ppermute | solution.py:556
  85.7 1.9 %collective-permute-start.1 = (bf16[6,16,256]{2,1,0:T(8,128)(2,1)}, bf16[6,16,256]{2,1,0:T(8,128)(2,1)S(1)}, u32[]{:S(2)}, u32[]{:S(2)}) collective-permute-start(bf16[6,16,256]{2,1,0:T(8,128)(2,1)} %get-tuple-element.26), channel_id=1, source_target_pairs={{1,0},{2,1},{3,2},{4,3},{5,4},{6,5},{7,6},{9,8},{10,9},{11,10},{12... | collective-permute-start | bytes 147464 | tf_op jit(solution)/shard_map/ppermute | solution.py:557
  87.6 0.0 copy-start.1
  87.7 1.0 %copy-done.1 = bf16[6,128,256]{2,1,0:T(8,128)(2,1)S(1)} copy-done((bf16[6,128,256]{2,1,0:T(8,128)(2,1)S(1)}, bf16[6,128,256]{2,1,0:T(8,128)(2,1)}, u32[]{:S(2)}) %copy-start.1) | copy-done | bytes 393240
  88.6 1.3 %score.1 = (bf16[6,128,256]{2,1,0:T(8,128)(2,1)}, f32[6,128,256]{2,1,0:T(8,128)}, f32[6,32,256]{2,1,0:T(8,128)S(1)}) custom-call(bf16[6,128,256]{2,1,0:T(8,128)(2,1)S(1)} %get-tuple-element.20.filt_ref, bf16[6,128,256]{2,1,0:T(8,128)(2,1)S(1)} %get-tuple-element.21.diff_ref, bf16[6,128,256]{2,1,0:T(8,128)(2,1)S(1)} %copy-done.1), custom_call_target="tpu_custom_call" | custom-call | tf_op jit(solution)/shard_map/score/pallas_call | solution.py:559
  90.0 0.0 collective-permute-done.above_ref
  90.0 2.8 %collective-permute-done.1.below_ref = bf16[6,16,256]{2,1,0:T(8,128)(2,1)S(1)} collective-permute-done((bf16[6,16,256]{2,1,0:T(8,128)(2,1)}, bf16[6,16,256]{2,1,0:T(8,128)(2,1)S(1)}, u32[]{:S(2)}, u32[]{:S(2)}) %collective-permute-start.1) | collective-permute-done | bytes 49184 | tf_op jit(solution)/shard_map/ppermute | solution.py:557
  92.8 0.9 edges.1
  (4 shorter events, 0.0 us)
Async XLA Ops:
  0.6 18.6 %copy-start.3 = (bf16[6,2,31]{2,1,0:T(2,128)(2,1)S(1)}, bf16[6,2,31]{2,1,0:T(2,128)(2,1)}, u32[]{:S(2)}) copy-start(bf16[6,2,31]{2,1,0:T(2,128)(2,1)} %param.17) | copy-start | bytes 2236
  0.6 19.1 %copy-start.2 = (f32[6,1,21,6]{2,1,3,0:T(1,128)S(1)}, f32[6,1,21,6]{2,1,3,0:T(1,128)}, u32[]{:S(2)}) copy-start(f32[6,1,21,6]{2,1,3,0:T(1,128)} %param.16) | copy-start | bytes 9076
  3.5 37.1 %all-to-all-start = ((bf16[64,40,128]{2,1,0:T(8,128)(2,1)}), bf16[64,40,128]{2,1,0:T(8,128)(2,1)S(1)}, u32[]{:S(2)}, u32[]{:S(2)}) async-start(bf16[64,40,128]{2,1,0:T(8,128)(2,1)} %bitcast.16), calls=%async_computation | async-start | bytes 1310720 | tf_op jit(solution)/shard_map/all_to_all | solution.py:481
  70.4 1.7 %copy-start = (bf16[3,384,1024]{2,1,0:T(8,128)(2,1)S(1)}, bf16[3,384,1024]{2,1,0:T(8,128)(2,1)}, u32[]{:S(2)}) copy-start(bf16[3,384,1024]{2,1,0:T(8,128)(2,1)} %get-tuple-element.17.down_ref) | copy-start | bytes 7077892
  77.7 12.3 %collective-permute-start = (bf16[6,16,256]{2,1,0:T(8,128)(2,1)}, bf16[6,16,256]{2,1,0:T(8,128)(2,1)S(1)}, u32[]{:S(2)}, u32[]{:S(2)}) collective-permute-start(bf16[6,16,256]{2,1,0:T(8,128)(2,1)} %get-tuple-element.25), channel_id=1, source_target_pairs={{0,1},{1,2},{2,3},{3,4},{4,5},{5,6},{6,7},{8,9},{9,10},{10,11},{11... | collective-permute-start | bytes 147464 | tf_op jit(solution)/shard_map/ppermute | solution.py:556
  85.7 7.1 %collective-permute-start.1 = (bf16[6,16,256]{2,1,0:T(8,128)(2,1)}, bf16[6,16,256]{2,1,0:T(8,128)(2,1)S(1)}, u32[]{:S(2)}, u32[]{:S(2)}) collective-permute-start(bf16[6,16,256]{2,1,0:T(8,128)(2,1)} %get-tuple-element.26), channel_id=1, source_target_pairs={{1,0},{2,1},{3,2},{4,3},{5,4},{6,5},{7,6},{9,8},{10,9},{11,10},{12... | collective-permute-start | bytes 147464 | tf_op jit(solution)/shard_map/ppermute | solution.py:557
  87.6 1.0 %copy-start.1 = (bf16[6,128,256]{2,1,0:T(8,128)(2,1)S(1)}, bf16[6,128,256]{2,1,0:T(8,128)(2,1)}, u32[]{:S(2)}) copy-start(bf16[6,128,256]{2,1,0:T(8,128)(2,1)} %get-tuple-element.22.rowf_any.rowf_ref) | copy-start | bytes 1179652

commit v5 on v3

--- a/solution.py
+++ b/solution.py
@@ -277,8 +277,8 @@
 
 def model_kernel(
     ox_ref, rows_ref, down_ref, across_any, far_any, colf_any, sci_any,
-    diff_any, filt_any, top_ref, bot_ref,
-    across_ref, far_ref, colf_ref, sci_ref, diff_ref, filt_ref, win_ref, stack_ref, sem, out_sem,
+    diff_any, filt_ref, top_ref, bot_ref,
+    across_ref, far_ref, colf_ref, sci_ref, diff_ref, win_ref, stack_ref, sem,
 ):
     whole = [
         pltpu.make_async_copy(src, dst, sem.at[k])
@@ -289,7 +289,7 @@
             )
         )
     ]
-    for copy in whole:
+    for copy in whole[:3]:
         copy.start()
     half = GROUP // 2
     move = gather_rows()
@@ -344,7 +344,6 @@
 
     col = lax.broadcasted_iota(jnp.int32, (SIDE, COLS), 1).astype(f32)
     tx = (2.0 * col + 1.0) / COLS - 1.0
-    out = []
 
     def spread(group):
         at = group[0] * 320
@@ -374,19 +373,13 @@
         top_ref[v] = filt[0:HALO]
         bot_ref[v] = filt[SIDE - HALO :]
 
-    def send(group, k, src, dst):
-        copy = pltpu.make_async_copy(
-            src.at[group[0] : group[-1] + 1], dst.at[group[0] : group[-1] + 1], out_sem.at[k]
-        )
-        copy.start()
-        out.append(copy)
-
     early, rest = (0, 1, 2), (3, 4, 5)
-    for v in early:
+    for v in (0, 1, 2, 3):
         window(v)
     whole[0].wait()
+    whole[3].start()
     spread(early)
-    for v in rest:
+    for v in (4, 5):
         window(v)
     spread(rest)
     for copy in whole[1:3]:
@@ -396,35 +389,32 @@
     for v in early:
         columns(v)
     whole[3].wait()
-    send(early, 0, diff_ref, diff_any)
-    send(early, 1, filt_ref, filt_any)
+    out = [
+        pltpu.make_async_copy(diff_ref.at[n : n + 3], diff_any.at[n : n + 3], sem.at[4 + n // 3])
+        for n in (0, 3)
+    ]
+    out[0].start()
     for v in rest:
         differ(v)
-    send(rest, 2, diff_ref, diff_any)
+    out[1].start()
     for v in rest:
         columns(v)
-    send(rest, 3, filt_ref, filt_any)
     for copy in out:
         copy.wait()
 
 
-def score_kernel(filt_any, rowf_any, score_any, part_ref, filt_ref, rowf_ref, score_ref, sem):
-    fetch = [
-        pltpu.make_async_copy(filt_any, filt_ref, sem.at[0]),
-        pltpu.make_async_copy(rowf_any, rowf_ref, sem.at[1]),
-    ]
-    for copy in fetch:
-        copy.start()
-    for copy in fetch:
-        copy.wait()
+def score_kernel(filt_ref, rowf_any, score_any, part_ref, rowf_ref, score_ref, sem):
+    rows = pltpu.make_async_copy(rowf_any, rowf_ref, sem.at[0])
+    rows.start()
+    rows.wait()
     for v in range(VISITS):
         score = jnp.dot(rowf_ref[v, :, 0:128], filt_ref[v], preferred_element_type=f32)
         score_ref[v] = score
         part_ref[v, 0:HALO] = score[0:HALO]
         part_ref[v, HALO:] = score[SIDE - HALO :]
-    out = pltpu.make_async_copy(score_ref, score_any, sem.at[2])
-    out.start()
-    out.wait()
+    done = pltpu.make_async_copy(score_ref, score_any, sem.at[1])
+    done.start()
+    done.wait()
 
 
 def edge_kernel(part_ref, above_ref, below_ref, rowf_ref, _, score_ref, buf_ref, sem):
@@ -530,10 +520,10 @@
     difference, filtered, top, bot = pl.pallas_call(
         model_kernel,
         in_specs=[SM, VM, VM] + [HB] * 4,
-        out_specs=[HB, HB, VM, VM],
+        out_specs=[HB, VM, VM, VM],
         out_shape=[
             sds((VISITS, SIDE, COLS), bf16),
-            sds((VISITS, SIDE, COLS), bf16),
+            pltpu.VMEM((VISITS, SIDE, COLS), bf16),
             sds((VISITS, HALO, COLS), bf16),
             sds((VISITS, HALO, COLS), bf16),
         ],
@@ -543,11 +533,9 @@
             pltpu.VMEM((VISITS, COLS, COLS), bf16),
             pltpu.VMEM((VISITS, SIDE, COLS), bf16),
             pltpu.VMEM((VISITS, SIDE, COLS), bf16),
-            pltpu.VMEM((VISITS, SIDE, COLS), bf16),
             pltpu.VMEM((VISITS * 320, 256), bf16),
             pltpu.VMEM((VISITS, LONG, COLS), bf16),
-            pltpu.SemaphoreType.DMA((4,)),
-            pltpu.SemaphoreType.DMA((4,)),
+            pltpu.SemaphoreType.DMA((6,)),
         ],
         name="model",
     )(ox, near(rows), near(down), jnp.asarray(across_band(taps)).astype(bf16), far, colf, science)
@@ -558,20 +546,20 @@
 
     score, part = pl.pallas_call(
         score_kernel,
-        in_specs=[HB, HB],
+        in_specs=[VM, HB],
         out_specs=[HB, VM],
         out_shape=[
             sds((VISITS, SIDE, COLS), f32),
             pltpu.VMEM((VISITS, 2 * HALO, COLS), f32),
         ],
         scratch_shapes=[
-            pltpu.VMEM((VISITS, SIDE, COLS), bf16),
             pltpu.VMEM((VISITS, SIDE, FAR), bf16),
             pltpu.VMEM((VISITS, SIDE, COLS), f32),
-            pltpu.SemaphoreType.DMA((3,)),
-        ],
+            pltpu.SemaphoreType.DMA((2,)),
+        ],
+        compiler_params=LIMIT,
         name="score",
-    )(filtered, rowf)
+    )(near(filtered), rowf)
 
     score = pl.pallas_call(
         edge_kernel,

time: 92.8 us -> 92.5 us (level)
  Pallas kernels: 28.3 us -> 27 us
  local copies, waits for them, and re-layouts: 1.21 us -> 2.19 us
    unnamed x7, local copies, waits for them, and re-layouts: 0.14 us -> 1.13 us
    pallas_call x1, Pallas kernels: 2.27 us -> 1.33 us  [body(): pl.pallas_call(score_kernel, in_specs=[VM, HB], out_specs=[HB, VM], out_s...]
  transfers between devices with their start and end apart: 3 -> 3, of which waited for: 2 -> 2; matrix products, arithmetic and copies ran while one was open for 2% -> 2% of each run, Pallas kernels for 18% -> 17%
where the time goes in v5:
time: 92.5 us; the launch traced here: 92.1 us
  blocking collectives  27.4 us (30%)
  Pallas kernels  27 us (29%)
  starting transfers between devices  25.8 us (28%)
  waiting for transfers between devices  8.21 us (9%)
  local copies, waits for them, and re-layouts  2.19 us (2%)
    all_to_all x1, blocking collectives, body(): rows = lax.all_to_all(picked, 'sky', 0, 0, tiled=True)  27.4 us
    all_to_all x1, starting transfers between devices, body(): lax.all_to_all(packed.reshape(GROUP, PACKED, 128), 'sky', 0, 0, tiled=True)  15.7 us
    pallas_call x1, Pallas kernels, body(): pl.pallas_call(bands_kernel, grid=(VISITS,), in_specs=[SM, SM, pl.BlockSp...  14 us
    ppermute x1, starting transfers between devices, body(): above = lax.ppermute(bot, 'ccd', [(i, i + 1) for i in range(count - 1)])  8.14 us
    pallas_call x1, Pallas kernels, body(): pl.pallas_call(model_kernel, in_specs=[SM, VM, VM] + [HB] * 4, out_specs=...  6.17 us
    all_to_all x1, waiting for transfers between devices, body(): lax.all_to_all(packed.reshape(GROUP, PACKED, 128), 'sky', 0, 0, tiled=True)  5.39 us
    ppermute x1, waiting for transfers between devices, body(): below = lax.ppermute(top, 'ccd', [(i + 1, i) for i in range(count - 1)])  2.82 us
    pallas_call x1, Pallas kernels, body(): pl.pallas_call(pack_kernel, out_shape=pltpu.VMEM((GROUP // 2, 2, PACKED,...  2.69 us
  transfers between devices with their start and end apart: 3, of which 2 were waited for; matrix products, arithmetic and copies ran while one was open for 2% of the time, Pallas kernels for 17%

profile of v5, /device:TPU:8, one launch (start us, length us, event | category | flops | bytes accessed | tf_op | source)
XLA Modules:
  0.0 92.1 jit_solution(748076392663495019)
XLA Ops:
  0.6 0.0 copy-start.2
  0.6 0.0 copy-start.1
  0.7 2.7 %pack.1 = bf16[32,2,40,128]{3,2,1,0:T(8,128)(2,1)} custom-call(bf16[16,128,128]{2,1,0:T(8,128)(2,1)} %cells_any.1, s32[1,36]{1,0:T(1,128)} %bitcast.21, s32[1,36]{1,0:T(1,128)} %index_any.1, s32[1,6]{1,0:T(1,128)} %bitcast.19, s32[1,6]{1,0:T(1,128)} %bitcast.17), custom_call_target="tpu_custom_call" | custom-call | tf_op jit(solution)/shard_map/pack/pallas_call | solution.py:453
  3.3 15.7 %all-to-all-start = ((bf16[64,40,128]{2,1,0:T(8,128)(2,1)}), bf16[64,40,128]{2,1,0:T(8,128)(2,1)S(1)}, u32[]{:S(2)}, u32[]{:S(2)}) async-start(bf16[64,40,128]{2,1,0:T(8,128)(2,1)} %bitcast.5), calls=%async_computation | async-start | bytes 1310720 | tf_op jit(solution)/shard_map/all_to_all | solution.py:469
  19.1 0.0 copy-done.2
  19.1 0.1 slice.27
  19.2 0.1 rev.4
  19.2 0.1 slice.28
  19.3 0.1 pad_slice_fusion.1
  19.4 0.1 maximum_bitcast_fusion
  19.5 0.1 pad_slice_fusion
  19.5 0.1 pad_maximum_fusion.1
  19.6 0.0 copy-done.1
  19.6 0.1 copy.16
  19.8 0.7 reshape.19.coef_ref
  20.4 0.6 pad_maximum_fusion.psf_ref
  21.1 14.0 %bands.1 = (bf16[3,384,1024]{2,1,0:T(8,128)(2,1)S(1)}, bf16[3,384,1024]{2,1,0:T(8,128)(2,1)}, bf16[6,256,256]{2,1,0:T(8,128)(2,1)}, bf16[6,128,256]{2,1,0:T(8,128)(2,1)}) custom-call(s32[6]{0:T(128)} %bitcast.20, f32[6,126]{1,0:T(8,128)} %reshape.19.coef_ref, f32[8,256]{1,0:T(8,128)} %constant.12.clone.taps_ref, f32[6,2,256]{2,1,0:T(2,128)} %pad_maximum_fusion.psf_ref), custom_call_target="tpu_custom_call" | custom-call | tf_op jit(solution)/shard_map/bands/pallas_call | solution.py:480
  35.1 5.4 %all-to-all-done.stripes_ref = bf16[64,40,128]{2,1,0:T(8,128)(2,1)S(1)} async-done(((bf16[64,40,128]{2,1,0:T(8,128)(2,1)}), bf16[64,40,128]{2,1,0:T(8,128)(2,1)S(1)}, u32[]{:S(2)}, u32[]{:S(2)}) %all-to-all-start) | async-done | bytes 655392 | tf_op jit(solution)/shard_map/all_to_all | solution.py:469
  40.5 1.9 %select.3 = bf16[64,40,128]{2,1,0:T(8,128)(2,1)S(1)} custom-call(s32[1]{0:T(128)} %bitcast.1.me_ref, bf16[64,40,128]{2,1,0:T(8,128)(2,1)S(1)} %all-to-all-done.stripes_ref), custom_call_target="tpu_custom_call" | custom-call | tf_op jit(solution)/shard_map/select/pallas_call | solution.py:509
  42.4 27.4 %all_to_all.10.rows_ref = bf16[64,40,128]{2,1,0:T(8,128)(2,1)S(1)} all-to-all(bf16[64,40,128]{2,1,0:T(8,128)(2,1)S(1)} %select.3), channel_id=1, replica_groups=mesh['sky'=64,'ccd'=8] {'sky'}, dimensions={0} | all-to-all | bytes 1310720 | tf_op jit(solution)/shard_map/all_to_all | solution.py:518
  69.8 6.2 %model.1 = (bf16[6,128,256]{2,1,0:T(8,128)(2,1)}, bf16[6,128,256]{2,1,0:T(8,128)(2,1)S(1)}, bf16[6,16,256]{2,1,0:T(8,128)(2,1)}, bf16[6,16,256]{2,1,0:T(8,128)(2,1)}) custom-call(s32[6]{0:T(128)} %bitcast.18, bf16[64,40,128]{2,1,0:T(8,128)(2,1)S(1)} %all_to_all.10.rows_ref, bf16[3,384,1024]{2,1,0:T(8,128)(2,1)S(1)} %get-tuple-element.16.down_ref, ...), custom_call_target="tpu_custom_call" | custom-call | tf_op jit(solution)/shard_map/model/pallas_call | solution.py:520
  76.0 8.1 %collective-permute-start = (bf16[6,16,256]{2,1,0:T(8,128)(2,1)}, bf16[6,16,256]{2,1,0:T(8,128)(2,1)S(1)}, u32[]{:S(2)}, u32[]{:S(2)}) collective-permute-start(bf16[6,16,256]{2,1,0:T(8,128)(2,1)} %get-tuple-element.23), channel_id=1, source_target_pairs={{0,1},{1,2},{2,3},{3,4},{4,5},{5,6},{6,7},{8,9},{9,10},{10,11},{11... | collective-permute-start | bytes 147464 | tf_op jit(solution)/shard_map/ppermute | solution.py:544
  84.1 1.9 %collective-permute-start.1 = (bf16[6,16,256]{2,1,0:T(8,128)(2,1)}, bf16[6,16,256]{2,1,0:T(8,128)(2,1)S(1)}, u32[]{:S(2)}, u32[]{:S(2)}) collective-permute-start(bf16[6,16,256]{2,1,0:T(8,128)(2,1)} %get-tuple-element.24), channel_id=1, source_target_pairs={{1,0},{2,1},{3,2},{4,3},{5,4},{6,5},{7,6},{9,8},{10,9},{11,10},{12... | collective-permute-start | bytes 147464 | tf_op jit(solution)/shard_map/ppermute | solution.py:545
  86.1 0.0 copy-start
  86.1 1.0 %copy-done = bf16[6,128,256]{2,1,0:T(8,128)(2,1)S(1)} copy-done((bf16[6,128,256]{2,1,0:T(8,128)(2,1)S(1)}, bf16[6,128,256]{2,1,0:T(8,128)(2,1)}, u32[]{:S(2)}) %copy-start) | copy-done | bytes 393240
  87.1 1.3 %score.1 = (f32[6,128,256]{2,1,0:T(8,128)}, f32[6,32,256]{2,1,0:T(8,128)S(1)}) custom-call(bf16[6,128,256]{2,1,0:T(8,128)(2,1)S(1)} %get-tuple-element.20.filt_ref, bf16[6,128,256]{2,1,0:T(8,128)(2,1)S(1)} %copy-done), custom_call_target="tpu_custom_call" | custom-call | tf_op jit(solution)/shard_map/score/pallas_call | solution.py:547
  88.4 0.0 collective-permute-done.above_ref
  88.4 2.8 %collective-permute-done.1.below_ref = bf16[6,16,256]{2,1,0:T(8,128)(2,1)S(1)} collective-permute-done((bf16[6,16,256]{2,1,0:T(8,128)(2,1)}, bf16[6,16,256]{2,1,0:T(8,128)(2,1)S(1)}, u32[]{:S(2)}, u32[]{:S(2)}) %collective-permute-start.1) | collective-permute-done | bytes 49184 | tf_op jit(solution)/shard_map/ppermute | solution.py:545
  91.2 0.9 edges.1
  (4 shorter events, 0.0 us)
Async XLA Ops:
  0.6 18.4 %copy-start.2 = (bf16[6,2,31]{2,1,0:T(2,128)(2,1)S(1)}, bf16[6,2,31]{2,1,0:T(2,128)(2,1)}, u32[]{:S(2)}) copy-start(bf16[6,2,31]{2,1,0:T(2,128)(2,1)} %param.17) | copy-start | bytes 2236
  0.6 19.0 %copy-start.1 = (f32[6,1,21,6]{2,1,3,0:T(1,128)S(1)}, f32[6,1,21,6]{2,1,3,0:T(1,128)}, u32[]{:S(2)}) copy-start(f32[6,1,21,6]{2,1,3,0:T(1,128)} %param.16) | copy-start | bytes 9076
  3.3 37.1 %all-to-all-start = ((bf16[64,40,128]{2,1,0:T(8,128)(2,1)}), bf16[64,40,128]{2,1,0:T(8,128)(2,1)S(1)}, u32[]{:S(2)}, u32[]{:S(2)}) async-start(bf16[64,40,128]{2,1,0:T(8,128)(2,1)} %bitcast.5), calls=%async_computation | async-start | bytes 1310720 | tf_op jit(solution)/shard_map/all_to_all | solution.py:469
  76.0 12.4 %collective-permute-start = (bf16[6,16,256]{2,1,0:T(8,128)(2,1)}, bf16[6,16,256]{2,1,0:T(8,128)(2,1)S(1)}, u32[]{:S(2)}, u32[]{:S(2)}) collective-permute-start(bf16[6,16,256]{2,1,0:T(8,128)(2,1)} %get-tuple-element.23), channel_id=1, source_target_pairs={{0,1},{1,2},{2,3},{3,4},{4,5},{5,6},{6,7},{8,9},{9,10},{10,11},{11... | collective-permute-start | bytes 147464 | tf_op jit(solution)/shard_map/ppermute | solution.py:544
  84.1 7.1 %collective-permute-start.1 = (bf16[6,16,256]{2,1,0:T(8,128)(2,1)}, bf16[6,16,256]{2,1,0:T(8,128)(2,1)S(1)}, u32[]{:S(2)}, u32[]{:S(2)}) collective-permute-start(bf16[6,16,256]{2,1,0:T(8,128)(2,1)} %get-tuple-element.24), channel_id=1, source_target_pairs={{1,0},{2,1},{3,2},{4,3},{5,4},{6,5},{7,6},{9,8},{10,9},{11,10},{12... | collective-permute-start | bytes 147464 | tf_op jit(solution)/shard_map/ppermute | solution.py:545
  86.1 1.0 %copy-start = (bf16[6,128,256]{2,1,0:T(8,128)(2,1)S(1)}, bf16[6,128,256]{2,1,0:T(8,128)(2,1)}, u32[]{:S(2)}) copy-start(bf16[6,128,256]{2,1,0:T(8,128)(2,1)} %get-tuple-element.21.rowf_any.rowf_ref) | copy-start | bytes 1179652

commit v6 on v5

--- a/solution.py
+++ b/solution.py
@@ -524,8 +524,8 @@
         out_shape=[
             sds((VISITS, SIDE, COLS), bf16),
             pltpu.VMEM((VISITS, SIDE, COLS), bf16),
-            sds((VISITS, HALO, COLS), bf16),
-            sds((VISITS, HALO, COLS), bf16),
+            pltpu.VMEM((VISITS, HALO, COLS), bf16),
+            pltpu.VMEM((VISITS, HALO, COLS), bf16),
         ],
         scratch_shapes=[
             pltpu.VMEM((FAR, 768), bf16),

time: 92.5 us -> 91.6 us (level)
  no operation moved by 1% of the time
where the time goes in v6:
time: 91.6 us; the launch traced here: 91.2 us
  blocking collectives  27.4 us (30%)
  Pallas kernels  26.3 us (29%)
  starting transfers between devices  25.8 us (28%)
  waiting for transfers between devices  8 us (9%)
  local copies, waits for them, and re-layouts  2.19 us (2%)
    all_to_all x1, blocking collectives, body(): rows = lax.all_to_all(picked, 'sky', 0, 0, tiled=True)  27.4 us
    all_to_all x1, starting transfers between devices, body(): lax.all_to_all(packed.reshape(GROUP, PACKED, 128), 'sky', 0, 0, tiled=True)  15.7 us
    pallas_call x1, Pallas kernels, body(): pl.pallas_call(bands_kernel, grid=(VISITS,), in_specs=[SM, SM, pl.BlockSp...  14 us
    ppermute x1, starting transfers between devices, body(): above = lax.ppermute(bot, 'ccd', [(i, i + 1) for i in range(count - 1)])  8.14 us
    pallas_call x1, Pallas kernels, body(): pl.pallas_call(model_kernel, in_specs=[SM, VM, VM] + [HB] * 4, out_specs=...  5.52 us
    all_to_all x1, waiting for transfers between devices, body(): lax.all_to_all(packed.reshape(GROUP, PACKED, 128), 'sky', 0, 0, tiled=True)  5.39 us
    pallas_call x1, Pallas kernels, body(): pl.pallas_call(pack_kernel, out_shape=pltpu.VMEM((GROUP // 2, 2, PACKED,...  2.69 us
    ppermute x1, waiting for transfers between devices, body(): below = lax.ppermute(top, 'ccd', [(i + 1, i) for i in range(count - 1)])  2.61 us
  transfers between devices with their start and end apart: 3, of which 2 were waited for; matrix products, arithmetic and copies ran while one was open for 2% of the time, Pallas kernels for 17%

profile of v6, /device:TPU:8, one launch (start us, length us, event | category | flops | bytes accessed | tf_op | source)
XLA Modules:
  0.0 91.2 jit_solution(8358078451967463077)
XLA Ops:
  0.6 0.0 copy-start.2
  0.6 0.0 copy-start.1
  0.7 2.7 %pack.1 = bf16[32,2,40,128]{3,2,1,0:T(8,128)(2,1)} custom-call(bf16[16,128,128]{2,1,0:T(8,128)(2,1)} %cells_any.1, s32[1,36]{1,0:T(1,128)} %bitcast.21, s32[1,36]{1,0:T(1,128)} %index_any.1, s32[1,6]{1,0:T(1,128)} %bitcast.19, s32[1,6]{1,0:T(1,128)} %bitcast.17), custom_call_target="tpu_custom_call" | custom-call | tf_op jit(solution)/shard_map/pack/pallas_call | solution.py:453
  3.3 15.7 %all-to-all-start = ((bf16[64,40,128]{2,1,0:T(8,128)(2,1)}), bf16[64,40,128]{2,1,0:T(8,128)(2,1)S(1)}, u32[]{:S(2)}, u32[]{:S(2)}) async-start(bf16[64,40,128]{2,1,0:T(8,128)(2,1)} %bitcast.5), calls=%async_computation | async-start | bytes 1310720 | tf_op jit(solution)/shard_map/all_to_all | solution.py:469
  19.1 0.0 copy-done.2
  19.1 0.1 slice.27
  19.2 0.1 rev.4
  19.2 0.1 slice.28
  19.3 0.1 pad_slice_fusion.1
  19.4 0.1 maximum_bitcast_fusion
  19.5 0.1 pad_slice_fusion
  19.5 0.1 pad_maximum_fusion.1
  19.6 0.0 copy-done.1
  19.6 0.1 copy.16
  19.8 0.7 reshape.19.coef_ref
  20.4 0.6 pad_maximum_fusion.psf_ref
  21.1 14.0 %bands.1 = (bf16[3,384,1024]{2,1,0:T(8,128)(2,1)S(1)}, bf16[3,384,1024]{2,1,0:T(8,128)(2,1)}, bf16[6,256,256]{2,1,0:T(8,128)(2,1)}, bf16[6,128,256]{2,1,0:T(8,128)(2,1)}) custom-call(s32[6]{0:T(128)} %bitcast.20, f32[6,126]{1,0:T(8,128)} %reshape.19.coef_ref, f32[8,256]{1,0:T(8,128)} %constant.12.clone.taps_ref, f32[6,2,256]{2,1,0:T(2,128)} %pad_maximum_fusion.psf_ref), custom_call_target="tpu_custom_call" | custom-call | tf_op jit(solution)/shard_map/bands/pallas_call | solution.py:480
  35.1 5.4 %all-to-all-done.stripes_ref = bf16[64,40,128]{2,1,0:T(8,128)(2,1)S(1)} async-done(((bf16[64,40,128]{2,1,0:T(8,128)(2,1)}), bf16[64,40,128]{2,1,0:T(8,128)(2,1)S(1)}, u32[]{:S(2)}, u32[]{:S(2)}) %all-to-all-start) | async-done | bytes 655392 | tf_op jit(solution)/shard_map/all_to_all | solution.py:469
  40.5 1.9 %select.3 = bf16[64,40,128]{2,1,0:T(8,128)(2,1)S(1)} custom-call(s32[1]{0:T(128)} %bitcast.1.me_ref, bf16[64,40,128]{2,1,0:T(8,128)(2,1)S(1)} %all-to-all-done.stripes_ref), custom_call_target="tpu_custom_call" | custom-call | tf_op jit(solution)/shard_map/select/pallas_call | solution.py:509
  42.4 27.4 %all_to_all.10.rows_ref = bf16[64,40,128]{2,1,0:T(8,128)(2,1)S(1)} all-to-all(bf16[64,40,128]{2,1,0:T(8,128)(2,1)S(1)} %select.3), channel_id=1, replica_groups=mesh['sky'=64,'ccd'=8] {'sky'}, dimensions={0} | all-to-all | bytes 1310720 | tf_op jit(solution)/shard_map/all_to_all | solution.py:518
  69.8 5.5 %model.1 = (bf16[6,128,256]{2,1,0:T(8,128)(2,1)}, bf16[6,128,256]{2,1,0:T(8,128)(2,1)S(1)}, bf16[6,16,256]{2,1,0:T(8,128)(2,1)S(1)}, bf16[6,16,256]{2,1,0:T(8,128)(2,1)S(1)}) custom-call(s32[6]{0:T(128)} %bitcast.18, bf16[64,40,128]{2,1,0:T(8,128)(2,1)S(1)} %all_to_all.10.rows_ref, bf16[3,384,1024]{2,1,0:T(8,128)(2,1)S(1)} %get-tuple-element.16.down_ref, ...), custom_call_target="tpu_custom_call" | custom-call | tf_op jit(solution)/shard_map/model/pallas_call | solution.py:520
  75.3 8.1 %collective-permute-start = (bf16[6,16,256]{2,1,0:T(8,128)(2,1)S(1)}, bf16[6,16,256]{2,1,0:T(8,128)(2,1)S(1)}, u32[]{:S(2)}, u32[]{:S(2)}) collective-permute-start(bf16[6,16,256]{2,1,0:T(8,128)(2,1)S(1)} %get-tuple-element.23), channel_id=1, source_target_pairs={{0,1},{1,2},{2,3},{3,4},{4,5},{5,6},{6,7},{8,9},{9,10},{10,11},{11... | collective-permute-start | bytes 147464 | tf_op jit(solution)/shard_map/ppermute | solution.py:544
  83.5 1.9 %collective-permute-start.1 = (bf16[6,16,256]{2,1,0:T(8,128)(2,1)S(1)}, bf16[6,16,256]{2,1,0:T(8,128)(2,1)S(1)}, u32[]{:S(2)}, u32[]{:S(2)}) collective-permute-start(bf16[6,16,256]{2,1,0:T(8,128)(2,1)S(1)} %get-tuple-element.24), channel_id=1, source_target_pairs={{1,0},{2,1},{3,2},{4,3},{5,4},{6,5},{7,6},{9,8},{10,9},{11,10},{12... | collective-permute-start | bytes 147464 | tf_op jit(solution)/shard_map/ppermute | solution.py:545
  85.4 0.0 copy-start
  85.4 1.0 %copy-done = bf16[6,128,256]{2,1,0:T(8,128)(2,1)S(1)} copy-done((bf16[6,128,256]{2,1,0:T(8,128)(2,1)S(1)}, bf16[6,128,256]{2,1,0:T(8,128)(2,1)}, u32[]{:S(2)}) %copy-start) | copy-done | bytes 393240
  86.4 1.3 %score.1 = (f32[6,128,256]{2,1,0:T(8,128)}, f32[6,32,256]{2,1,0:T(8,128)S(1)}) custom-call(bf16[6,128,256]{2,1,0:T(8,128)(2,1)S(1)} %get-tuple-element.20.filt_ref, bf16[6,128,256]{2,1,0:T(8,128)(2,1)S(1)} %copy-done), custom_call_target="tpu_custom_call" | custom-call | tf_op jit(solution)/shard_map/score/pallas_call | solution.py:547
  87.7 0.0 collective-permute-done.above_ref
  87.8 2.6 %collective-permute-done.1.below_ref = bf16[6,16,256]{2,1,0:T(8,128)(2,1)S(1)} collective-permute-done((bf16[6,16,256]{2,1,0:T(8,128)(2,1)S(1)}, bf16[6,16,256]{2,1,0:T(8,128)(2,1)S(1)}, u32[]{:S(2)}, u32[]{:S(2)}) %collective-permute-start.1) | collective-permute-done | bytes 49184 | tf_op jit(solution)/shard_map/ppermute | solution.py:545
  90.4 0.9 edges.1
  (4 shorter events, 0.0 us)
Async XLA Ops:
  0.6 18.4 %copy-start.2 = (bf16[6,2,31]{2,1,0:T(2,128)(2,1)S(1)}, bf16[6,2,31]{2,1,0:T(2,128)(2,1)}, u32[]{:S(2)}) copy-start(bf16[6,2,31]{2,1,0:T(2,128)(2,1)} %param.17) | copy-start | bytes 2236
  0.6 19.0 %copy-start.1 = (f32[6,1,21,6]{2,1,3,0:T(1,128)S(1)}, f32[6,1,21,6]{2,1,3,0:T(1,128)}, u32[]{:S(2)}) copy-start(f32[6,1,21,6]{2,1,3,0:T(1,128)} %param.16) | copy-start | bytes 9076
  3.3 37.1 %all-to-all-start = ((bf16[64,40,128]{2,1,0:T(8,128)(2,1)}), bf16[64,40,128]{2,1,0:T(8,128)(2,1)S(1)}, u32[]{:S(2)}, u32[]{:S(2)}) async-start(bf16[64,40,128]{2,1,0:T(8,128)(2,1)} %bitcast.5), calls=%async_computation | async-start | bytes 1310720 | tf_op jit(solution)/shard_map/all_to_all | solution.py:469
  75.3 12.4 %collective-permute-start = (bf16[6,16,256]{2,1,0:T(8,128)(2,1)S(1)}, bf16[6,16,256]{2,1,0:T(8,128)(2,1)S(1)}, u32[]{:S(2)}, u32[]{:S(2)}) collective-permute-start(bf16[6,16,256]{2,1,0:T(8,128)(2,1)S(1)} %get-tuple-element.23), channel_id=1, source_target_pairs={{0,1},{1,2},{2,3},{3,4},{4,5},{5,6},{6,7},{8,9},{9,10},{10,11},{11... | collective-permute-start | bytes 147464 | tf_op jit(solution)/shard_map/ppermute | solution.py:544
  83.5 6.9 %collective-permute-start.1 = (bf16[6,16,256]{2,1,0:T(8,128)(2,1)S(1)}, bf16[6,16,256]{2,1,0:T(8,128)(2,1)S(1)}, u32[]{:S(2)}, u32[]{:S(2)}) collective-permute-start(bf16[6,16,256]{2,1,0:T(8,128)(2,1)S(1)} %get-tuple-element.24), channel_id=1, source_target_pairs={{1,0},{2,1},{3,2},{4,3},{5,4},{6,5},{7,6},{9,8},{10,9},{11,10},{12... | collective-permute-start | bytes 147464 | tf_op jit(solution)/shard_map/ppermute | solution.py:545
  85.4 1.0 %copy-start = (bf16[6,128,256]{2,1,0:T(8,128)(2,1)S(1)}, bf16[6,128,256]{2,1,0:T(8,128)(2,1)}, u32[]{:S(2)}) copy-start(bf16[6,128,256]{2,1,0:T(8,128)(2,1)} %get-tuple-element.21.rowf_any.rowf_ref) | copy-start | bytes 1179652
